TPU v7x, 32 devices: a whole 2x2x4 slice. The times are simulated.
32 devices in a mesh: ctx: 8 (over z, x), tp: 4 (over y, core).
Axes of the slice: x: 2, y: 2, z: 4, core: 2. Of those that a mesh axis runs over, the one named last changes fastest.
Arguments:
- query: bfloat16 [4096, 5120], P(('ctx', 'tp')), may hold values from -5 to 5
- key_in: bfloat16 [4096, 5120], P(('ctx', 'tp')), may hold values from -5 to 5
- value_in: bfloat16 [4096, 5120], P(('ctx', 'tp')), may hold values from -6 to 6
- out_grad: bfloat16 [4096, 5120], P(('ctx', 'tp')), may hold values from -18 to 18
- lengths: int32 [32], replicated, may hold values from 1 to 512, 4096 in all
Outputs:
- query_grad: bfloat16 [4096, 5120], P(('ctx', 'tp'))
- key_grad: bfloat16 [4096, 5120], P(('ctx', 'tp'))
- value_grad: bfloat16 [4096, 5120], P(('ctx', 'tp'))
Inputs may be any that keep to these rules, and one draw needn't show every extreme that they name: lengths[p] is the number of residues of protein p; proteins follow one another in list order, the lengths sum to 4096, and the longest has exactly 512 residues.
All inputs are finite; a program needn't handle non-finite values.
Results may differ from a plain program's by a relative error of at most 0.019.
Values may be sent and summed in bfloat16 or wider, within the bound.
No kernel may reach another device: no remote copies, remote signals or barrier semaphores. Data moves between devices by JAX's collectives and lax.ppermute only.
A program may use at most 192 MiB of HBM per device.

v0:
```python
import jax
import jax.numpy as jnp
from jax import lax
from jax.sharding import PartitionSpec as P

HEAD_DIM = 128


NEG = -1e30


def extended(cells, sides, width):
    for axis, dim in sides:
        count = lax.axis_size(axis)
        ends = count - 1
        head = lax.slice_in_dim(cells, 0, width, axis=dim)
        tail = lax.slice_in_dim(cells, cells.shape[dim] - width, cells.shape[dim], axis=dim)
        cells = jnp.concatenate(
            [
                lax.ppermute(tail, axis, [(i, (i + 1) % count) for i in range(ends)]),
                cells,
                lax.ppermute(head, axis, [((i + 1) % count, i) for i in range(ends)]),
            ],
            axis=dim,
        )
    return cells


def segment_ids(lengths, first, count):
    bounds = jnp.cumsum(lengths)
    positions = first + jnp.arange(count, dtype=jnp.int32)
    inside = jnp.sum((bounds[None, :] <= positions[:, None]).astype(jnp.int32), axis=1)
    return jnp.where(positions < 0, -1, inside)


def masked_scores(queries, keys, seg_rows, seg_cols, scale):
    raw = jnp.einsum("qhd,khd->hqk", queries, keys, preferred_element_type=jnp.float32) * scale
    return jnp.where(seg_rows[None, :, None] == seg_cols[None, None, :], raw, NEG)


def key_terms(dscore, probs_b, queries, grads_out, scale):
    key_term = (
        jnp.einsum("hqk,qhd->khd", dscore, queries, preferred_element_type=jnp.float32) * scale
    )
    value_term = jnp.einsum("hqk,qhd->khd", probs_b, grads_out, preferred_element_type=jnp.float32)
    return (key_term.reshape(key_term.shape[0], -1), value_term.reshape(value_term.shape[0], -1))


def shards(query, key_in, value_in, out_grad, lengths):
    by_heads = (
        lax.all_to_all(query, "tp", split_axis=1, concat_axis=0, tiled=True),
        lax.all_to_all(key_in, "tp", split_axis=1, concat_axis=0, tiled=True),
        lax.all_to_all(value_in, "tp", split_axis=1, concat_axis=0, tiled=True),
        lax.all_to_all(out_grad, "tp", split_axis=1, concat_axis=0, tiled=True),
    )
    rows = by_heads[0].shape[0]
    width = by_heads[0].shape[1]
    heads = width // HEAD_DIM
    scale = HEAD_DIM ** (-0.5)
    queries = by_heads[0].reshape(rows, heads, HEAD_DIM)
    grads_out = by_heads[3].reshape(rows, heads, HEAD_DIM)
    start = lax.axis_index("ctx") * rows
    seg_all = segment_ids(lengths, start - rows, 3 * rows)
    seg_own = seg_all[rows : 2 * rows]
    kv_wide = extended(jnp.stack((by_heads[1], by_heads[2])), (("ctx", 1),), rows)
    pieces = []
    for block_place in (1, 0, 2):
        low = block_place * rows
        key_piece = kv_wide[0, low : low + rows].reshape(rows, heads, HEAD_DIM)
        value_piece = kv_wide[1, low : low + rows].reshape(rows, heads, HEAD_DIM)
        pieces.append((block_place, key_piece, value_piece, seg_all[low : low + rows]))
    row_top = jnp.full((heads, rows), NEG, jnp.float32)
    row_total = jnp.zeros((heads, rows), jnp.float32)
    kept_scores = []
    for block_place, key_piece, value_piece, piece_seg in pieces:
        scores = masked_scores(queries, key_piece, seg_own, piece_seg, scale)
        kept_scores.append(None)
        new_top = jnp.maximum(row_top, jnp.max(scores, axis=2))
        row_total = row_total * jnp.exp(row_top - new_top) + jnp.sum(
            jnp.exp(scores - new_top[:, :, None]), axis=2
        )
        row_top = new_top
    log_total = row_top + jnp.log(row_total)
    row_dot = jnp.zeros((heads, rows), jnp.float32)
    kept_dprob = []
    for number, (block_place, key_piece, value_piece, piece_seg) in enumerate(pieces):
        scores = masked_scores(queries, key_piece, seg_own, piece_seg, scale)
        probs_b = jnp.exp(scores - log_total[:, :, None]).astype(jnp.bfloat16)
        dprob = jnp.einsum(
            "qhd,khd->hqk", grads_out, value_piece, preferred_element_type=jnp.float32
        )
        kept_dprob.append(None)
        row_dot = row_dot + jnp.sum(probs_b.astype(jnp.float32) * dprob, axis=2)
    query_sum = jnp.zeros((rows, heads, HEAD_DIM), jnp.float32)
    own_terms = None
    for number, (block_place, key_piece, value_piece, piece_seg) in enumerate(pieces):
        scores = masked_scores(queries, key_piece, seg_own, piece_seg, scale)
        dprob = jnp.einsum(
            "qhd,khd->hqk", grads_out, value_piece, preferred_element_type=jnp.float32
        )
        probs = jnp.exp(scores - log_total[:, :, None])
        probs_b = probs.astype(jnp.bfloat16)
        dscore = (probs * (dprob - row_dot[:, :, None])).astype(jnp.bfloat16)
        query_sum = query_sum + jnp.einsum(
            "hqk,khd->qhd", dscore, key_piece, preferred_element_type=jnp.float32
        )
        if block_place == 1:
            own_terms = key_terms(dscore, probs_b, queries, grads_out, scale)
    qg_wide = extended(jnp.stack((by_heads[0], by_heads[3])), (("ctx", 1),), rows)
    stat_wide = extended(jnp.stack((log_total, row_dot)), (("ctx", 2),), rows)
    key_sum = own_terms[0]
    value_sum = own_terms[1]
    own_keys = pieces[0][1]
    own_values = pieces[0][2]
    for block_place in (0, 2):
        low = block_place * rows
        side_queries = qg_wide[0, low : low + rows].reshape(rows, heads, HEAD_DIM)
        side_grads = qg_wide[1, low : low + rows].reshape(rows, heads, HEAD_DIM)
        side_total = stat_wide[0, :, low : low + rows]
        side_dot = stat_wide[1, :, low : low + rows]
        scores = masked_scores(side_queries, own_keys, seg_all[low : low + rows], seg_own, scale)
        probs = jnp.exp(scores - side_total[:, :, None])
        probs_b = probs.astype(jnp.bfloat16)
        dprob = jnp.einsum(
            "qhd,khd->hqk", side_grads, own_values, preferred_element_type=jnp.float32
        )
        dscore = (probs * (dprob - side_dot[:, :, None])).astype(jnp.bfloat16)
        terms = key_terms(dscore, probs_b, side_queries, side_grads, scale)
        key_sum = key_sum + terms[0]
        value_sum = value_sum + terms[1]
    query_grad = (query_sum * scale).reshape(rows, width).astype(jnp.bfloat16)
    back = (
        lax.all_to_all(query_grad, "tp", split_axis=0, concat_axis=1, tiled=True),
        lax.all_to_all(key_sum.astype(jnp.bfloat16), "tp", split_axis=0, concat_axis=1, tiled=True),
        lax.all_to_all(
            value_sum.astype(jnp.bfloat16), "tp", split_axis=0, concat_axis=1, tiled=True
        ),
    )
    return (back[0], back[1], back[2])


def solution(mesh):
    placed = (
        P(("ctx", "tp"), None),
        P(("ctx", "tp"), None),
        P(("ctx", "tp"), None),
        P(("ctx", "tp"), None),
        P(),
    )
    return jax.shard_map(
        shards,
        mesh=mesh,
        in_specs=placed,
        out_specs=(P(("ctx", "tp"), None), P(("ctx", "tp"), None), P(("ctx", "tp"), None)),
        check_vma=False,
    )
```

profile of v0, /device:TPU:0, one launch (start us, length us, event | category | flops | bytes accessed | tf_op | source)
XLA Modules:
  0.0 488.0 jit_solution(4495784961664027285)
XLA Ops:
  8.9 15.8 %all-to-all-done.2 = bf16[128,4,1280]{0,2,1:T(8,128)(2,1)S(1)} async-done(((bf16[128,4,1280]{0,2,1:T(8,128)(2,1)}), bf16[128,4,1280]{0,2,1:T(8,128)(2,1)S(1)}, u32[]{:S(2)}, u32[]{:S(2)}) %all-to-all-start.2) | async-done | bytes 1310752 | tf_op jit(solution)/shard_map/all_to_all | solution.py:53
  30.6 14.8 %all-to-all-done.1 = bf16[128,4,1280]{0,2,1:T(8,128)(2,1)S(1)} async-done(((bf16[128,4,1280]{0,2,1:T(8,128)(2,1)}), bf16[128,4,1280]{0,2,1:T(8,128)(2,1)S(1)}, u32[]{:S(2)}, u32[]{:S(2)}) %all-to-all-start.1) | async-done | bytes 1310752 | tf_op jit(solution)/shard_map/all_to_all | solution.py:52
  56.2 5.7 %collective-permute-start = (bf16[2,512,1280]{2,1,0:T(8,128)(2,1)}, bf16[2,512,1280]{2,1,0:T(8,128)(2,1)}, u32[]{:S(2)}, u32[]{:S(2)}) collective-permute-start(bf16[2,512,1280]{2,1,0:T(8,128)(2,1)} %pad_maximum_fusion), channel_id=1, source_target_pairs={{0,4},{4,8},{8,12},{12,16},{16,20},{20,24},{24,28},{1,5},{5,9},{9,... | collective-permute-start | bytes 7864328 | tf_op jit(solution)/shard_map/ppermute | solution.py:20
  75.8 6.5 %copy.298 = bf16[4,128,1280]{1,0,2:T(4,128)(2,1)S(1)} copy(bf16[4,128,1280]{1,2,0:T(8,128)(2,1)} %bitcast.2) | data formatting | bytes 2621440 | tf_op jit(solution)/shard_map/all_to_all | solution.py:51
  89.0 7.4 %copy.300 = bf16[4,128,1280]{1,0,2:T(4,128)(2,1)} copy(bf16[4,128,1280]{1,2,0:T(8,128)(2,1)} %bitcast.201) | data formatting | bytes 2621440 | tf_op jit(solution)/shard_map/all_to_all | solution.py:52
  96.3 6.9 %copy.319 = bf16[4,128,1280]{1,0,2:T(4,128)(2,1)} copy(bf16[4,128,1280]{1,2,0:T(8,128)(2,1)S(1)} %bitcast.199) | data formatting | bytes 2621440 | tf_op jit(solution)/shard_map/all_to_all | solution.py:53
  103.2 6.7 %copy.318 = bf16[4,128,1280]{1,0,2:T(4,128)(2,1)S(1)} copy(bf16[4,128,1280]{1,2,0:T(8,128)(2,1)} %bitcast.14) | data formatting | bytes 2621440 | tf_op jit(solution)/shard_map/all_to_all | solution.py:54
  115.1 6.3 %collective-permute-start.2 = (bf16[2,512,1280]{1,2,0:T(8,128)(2,1)}, bf16[2,512,1280]{1,2,0:T(8,128)(2,1)}, u32[]{:S(2)}, u32[]{:S(2)}) collective-permute-start(bf16[2,512,1280]{1,2,0:T(8,128)(2,1)} %constant_dynamic-update-slice_fusion), channel_id=1, source_target_pairs={{0,4},{4,8},{8,12},{12,16},{16,20},{20,24},{24,28},{1,5},{5,9},{9,... | collective-permute-start | bytes 7864328 | tf_op jit(solution)/shard_map/ppermute | solution.py:20
  129.1 7.2 %fusion.74 = f32[10,512,512]{1,2,0:T(8,128)} fusion(bf16[512,10,128]{0,2,1:T(8,128)(2,1)} %reshape.387, bf16[512,10,128]{0,2,1:T(8,128)(2,1)} %reshape_squeeze_stack.7), kind=kOutput, calls=%fused_computation.114 | convolution fusion | flops 671088640 | bytes 13107200 | tf_op jit(solution)/shard_map/qhd,khd->hqk/dot_general | solution.py:98
  136.4 6.1 %fusion.11 = (f32[10,512]{1,0:T(8,128)S(1)}, f32[10,512,512]{1,2,0:T(8,128)}) fusion(pred[512,512]{0,1:T(8,128)(4,1)S(1)} %get-tuple-element.42, bf16[512,10,128]{0,2,1:T(8,128)(2,1)S(1)} %reshape.386, bf16[512,10,128]{0,2,1:T(8,128)(2,1)S(1)} %reshape_squeeze_stack.6), kind=kOutput, calls=%fused_computation.31 | convolution fusion | flops 678947840 | bytes 13389824 | tf_op jit(solution)/shard_map/qhd,khd->hqk/dot_general | solution.py:37
  142.4 87.8 %collective-permute-done = bf16[2,512,1280]{2,1,0:T(8,128)(2,1)} collective-permute-done((bf16[2,512,1280]{2,1,0:T(8,128)(2,1)}, bf16[2,512,1280]{2,1,0:T(8,128)(2,1)}, u32[]{:S(2)}, u32[]{:S(2)}) %collective-permute-start) | collective-permute-done | bytes 2621472 | tf_op jit(solution)/shard_map/ppermute | solution.py:20
  235.2 5.4 %multiply_bitcast_fusion = f32[10,512,512]{2,1,0:T(8,128)} fusion(bf16[512,10,128]{0,2,1:T(8,128)(2,1)S(1)} %bitcast.196, bf16[512,10,128]{0,2,1:T(8,128)(2,1)S(1)} %reshape.386), kind=kOutput, calls=%fused_computation.23 | convolution fusion | flops 673710080 | bytes 13107200 | tf_op jit(solution)/shard_map/qhd,khd->hqk/dot_general | solution.py:37
  240.6 11.2 %copy.310 = f32[10,512,512]{1,2,0:T(8,128)} copy(f32[10,512,512]{2,1,0:T(8,128)} %multiply_bitcast_fusion) | data formatting | bytes 20971520 | tf_op jit(solution)/shard_map/mul | solution.py:37
  256.9 6.2 %fusion.73 = (f32[10,512]{1,0:T(8,128)S(1)}, f32[10,512,512]{2,1,0:T(8,128)}) fusion(bf16[512,10,128]{0,2,1:T(8,128)(2,1)S(1)} %bitcast.194, bf16[512,10,128]{0,2,1:T(8,128)(2,1)S(1)} %reshape.386, pred[512,512]{1,0:T(8,128)(4,1)S(1)} %copy-done.17), kind=kOutput, calls=%fused_computation.113 | convolution fusion | flops 678947840 | bytes 13389824 | tf_op jit(solution)/shard_map/qhd,khd->hqk/dot_general | solution.py:37
  263.1 11.3 %copy.325 = f32[10,512,512]{1,2,0:T(8,128)} copy(f32[10,512,512]{2,1,0:T(8,128)} %get-tuple-element.44) | data formatting | bytes 20971520 | tf_op jit(solution)/shard_map/jit(_where)/select_n | solution.py:38
  274.4 5.6 %select_reduce_fusion = f32[10,512]{1,0:T(8,128)S(1)} fusion(f32[10,512,512]{1,2,0:T(8,128)} %copy.310, pred[512,512]{0,1:T(8,128)(4,1)S(1)} %copy-done.10), kind=kLoop, calls=%fused_computation.28 | loop fusion | flops 5237760 | bytes 10768384 | tf_op jit(solution)/shard_map/reduce_max | solution.py:78
  280.7 6.2 %exponential_reduce_fusion = f32[10,512]{1,0:T(8,128)} fusion(f32[10,512,512]{2,1,0:T(8,128)} %get-tuple-element.44, f32[10,512]{1,0:T(8,128)S(1)} %get-tuple-element.18), kind=kLoop, calls=%fused_computation.20 | loop fusion | flops 5237760 | bytes 10526720 | tf_op jit(solution)/shard_map/reduce_sum | solution.py:79
  296.2 6.9 %fusion.75 = f32[10,512,512]{2,1,0:T(8,128)} fusion(bf16[512,10,128]{0,2,1:T(8,128)(2,1)} %bitcast.208, bf16[512,10,128]{0,2,1:T(8,128)(2,1)S(1)} %copy-done.3), kind=kOutput, calls=%fused_computation.115 | convolution fusion | flops 671088640 | bytes 13107200 | tf_op jit(solution)/shard_map/qhd,khd->hqk/dot_general | solution.py:89
  305.5 23.3 %fusion.3 = (f32[10,512]{1,0:T(8,128)S(1)}, f32[10,512]{1,0:T(8,128)S(1)}, f32[10,512]{1,0:T(8,128)S(1)}, f32[10,512,512]{2,1,0:T(8,128)}) fusion(f32[10,512,512]{1,2,0:T(8,128)} %copy.310, f32[10,512]{1,0:T(8,128)S(1)} %log_add_fusion, pred[512,512]{0,1:T(8,128)(4,1)S(1)} %copy-done.11, f32[10,512,512]{2,1,0:T(8,128)} %fusion.75, ...), kind=kOutput, calls=%fused_computation.7 | convolution fusion | flops 718259200 | bytes 66142208 | tf_op jit(solution)/shard_map/qhd,khd->hqk/dot_general | solution.py:89
  328.9 9.3 %multiply_convert_fusion.2 = bf16[10,512,512]{1,2,0:T(8,128)(2,1)S(1)} fusion(f32[10,512,512]{1,2,0:T(8,128)} %fusion.74, f32[10,512,512]{1,2,0:T(8,128)} %get-tuple-element.46, f32[10,512]{1,0:T(8,128)S(1)} %add_add_fusion, f32[10,512]{1,0:T(8,128)S(1)} %log_add_fusion, pred[512,512]{0,1:T(8,128)(4,1)S(1)} %get-tuple-element.42), kind=kLoop, calls=%fused_computation.15 | loop fusion | flops 15728640 | bytes 26517504 | tf_op jit(solution)/shard_map/convert_element_type | solution.py:103
  338.8 5.0 %collective-permute-start.3 = (f32[2,10,512]{2,1,0:T(8,128)}, f32[2,10,512]{2,1,0:T(8,128)}, u32[]{:S(2)}, u32[]{:S(2)}) collective-permute-start(f32[2,10,512]{2,1,0:T(8,128)} %pad_maximum_fusion.1), channel_id=1, source_target_pairs={{0,4},{4,8},{8,12},{12,16},{16,20},{20,24},{24,28},{1,5},{5,9},{9,... | collective-permute-start | bytes 122888 | tf_op jit(solution)/shard_map/ppermute | solution.py:20
  348.8 9.7 %fusion.26 = f32[10,128,512]{1,2,0:T(8,128)} fusion(bf16[512,10,128]{0,2,1:T(8,128)(2,1)} %bitcast.197, f32[10,512,512]{2,1,0:T(8,128)} %get-tuple-element.47, f32[10,512,512]{1,2,0:T(8,128)S(1)} %bitcast.189, f32[10,512]{1,0:T(8,128)S(1)} %add_add_fusion, f32[10,512]{1,0:T(8,128)S(1)} %log_add_fusion, pred[512,512]{0,1:T(8,128)(4,1)S(1)} %copy-done.11), kind=kOutput, calls=%fused_computation.43 | convolution fusion | flops 684195840 | bytes 25206784 | tf_op jit(solution)/shard_map/hqk,khd->qhd/dot_general | solution.py:104
  358.5 12.6 %fusion.42 = bf16[512,10,128]{2,0,1:T(8,128)(2,1)} fusion(f32[10,128,512]{1,2,0:T(8,128)} %fusion.26, f32[10,512,128]{2,1,0:T(8,128)} %fusion.76, bf16[512,10,128]{0,2,1:T(8,128)(2,1)S(1)} %bitcast.195, f32[10,512,512]{2,1,0:T(8,128)} %fusion.75, f32[10,512,512]{1,2,0:T(8,128)} %copy.325, f32[10,512]{1,0:T(8,128)S(1)} %add_add_fusion, ...), kind=kOutput, calls=%fused_computation.62 | convolution fusion | flops 684195840 | bytes 28876800 | tf_op jit(solution)/shard_map/hqk,khd->qhd/dot_general | solution.py:104
  379.7 4.5 all-to-all-start.4
  384.2 5.7 %fusion.77 = f32[10,512,128]{2,1,0:T(8,128)} fusion(bf16[10,512,512]{1,2,0:T(8,128)(2,1)} %copy-done, bf16[512,10,128]{0,2,1:T(8,128)(2,1)S(1)} %reshape.386), kind=kOutput, calls=%fused_computation.117 | convolution fusion | flops 671088640 | bytes 9175040 | tf_op jit(solution)/shard_map/hqk,qhd->khd/dot_general | solution.py:43
  392.9 5.4 %fusion.78 = f32[10,512,512]{1,2,0:T(8,128)} fusion(bf16[512,10,128]{0,2,1:T(8,128)(2,1)S(1)} %bitcast.204, bf16[512,10,128]{0,2,1:T(8,128)(2,1)S(1)} %copy-done.2), kind=kOutput, calls=%fused_computation.118 | convolution fusion | flops 671088640 | bytes 13107200 | tf_op jit(solution)/shard_map/qhd,khd->hqk/dot_general | solution.py:37
  405.4 5.6 %fusion.79 = f32[10,512,512]{1,2,0:T(8,128)} fusion(bf16[512,10,128]{0,2,1:T(8,128)(2,1)S(1)} %bitcast.202, bf16[512,10,128]{0,2,1:T(8,128)(2,1)S(1)} %copy-done.2), kind=kOutput, calls=%fused_computation.119 | convolution fusion | flops 671088640 | bytes 13107200 | tf_op jit(solution)/shard_map/qhd,khd->hqk/dot_general | solution.py:37
  411.7 11.4 %fusion.28 = f32[10,128,512]{1,2,0:T(8,128)} fusion(bf16[512,10,128]{0,2,1:T(8,128)(2,1)} %bitcast.205, f32[10,512,512]{1,2,0:T(8,128)} %fusion.78, f32[10,512]{1,0:T(8,128)S(1)} %get-tuple-element.31, f32[10,512]{1,0:T(8,128)S(1)} %get-tuple-element.30, pred[512,512]{0,1:T(8,128)(4,1)S(1)} %copy-done.31, bf16[512,10,128]{0,2,1:T(8,128)(2,1)} %bitcast.216, ...), kind=kOutput, calls=%fused_computation.44 | convolution fusion | flops 1357905920 | bytes 17342464 | tf_op jit(solution)/shard_map/hqk,qhd->khd/dot_general | solution.py:43
  424.0 9.3 %fusion.40 = bf16[512,10,128]{2,0,1:T(8,128)(2,1)} fusion(f32[10,128,512]{1,2,0:T(8,128)} %fusion.28, f32[10,512,128]{2,1,0:T(8,128)} %fusion.77, bf16[512,10,128]{0,2,1:T(8,128)(2,1)S(1)} %bitcast.203, f32[10,512,512]{1,2,0:T(8,128)} %fusion.79, f32[10,512]{1,0:T(8,128)S(1)} %get-tuple-element.29, f32[10,512]{1,0:T(8,128)S(1)} %get-tuple-element.28, ...), kind=kOutput, calls=%fused_computation.58 | convolution fusion | flops 1361838080 | bytes 21274624 | tf_op jit(solution)/shard_map/hqk,qhd->khd/dot_general | solution.py:43
  436.5 8.4 %fusion.14 = f32[10,128,512]{1,2,0:T(8,128)} fusion(bf16[512,10,128]{0,2,1:T(8,128)(2,1)} %bitcast.217, f32[10,512,512]{1,2,0:T(8,128)} %fusion.78, f32[10,512]{1,0:T(8,128)S(1)} %get-tuple-element.30, pred[512,512]{0,1:T(8,128)(4,1)S(1)} %copy-done.31), kind=kOutput, calls=%fused_computation.33 | convolution fusion | flops 681574400 | bytes 14700544 | tf_op jit(solution)/shard_map/hqk,qhd->khd/dot_general | solution.py:45
  448.4 9.5 %fusion.39 = bf16[512,10,128]{2,0,1:T(8,128)(2,1)} fusion(f32[10,128,512]{1,2,0:T(8,128)} %fusion.14, f32[10,512,128]{2,1,0:T(8,128)} %fusion.64, bf16[512,10,128]{0,2,1:T(8,128)(2,1)S(1)} %bitcast.215, f32[10,512,512]{1,2,0:T(8,128)} %fusion.79, f32[10,512]{1,0:T(8,128)S(1)} %get-tuple-element.28, pred[512,512]{0,1:T(8,128)(4,1)S(1)} %copy-done.30), kind=kOutput, calls=%fused_computation.55 | convolution fusion | flops 683540480 | bytes 18632704 | tf_op jit(solution)/shard_map/hqk,qhd->khd/dot_general | solution.py:45
  473.0 13.3 %all-to-all-done.6 = bf16[4,128,1280]{1,2,0:T(8,128)(2,1)S(1)} async-done(((bf16[4,128,1280]{1,2,0:T(8,128)(2,1)}), bf16[4,128,1280]{1,2,0:T(8,128)(2,1)S(1)}, u32[]{:S(2)}, u32[]{:S(2)}) %all-to-all-start.6) | async-done | bytes 1310752 | tf_op jit(solution)/shard_map/all_to_all | solution.py:135
  (167 shorter events, 129.6 us)
Async XLA Ops:
  3.2 21.5 %all-to-all-start.2 = ((bf16[128,4,1280]{0,2,1:T(8,128)(2,1)}), bf16[128,4,1280]{0,2,1:T(8,128)(2,1)S(1)}, u32[]{:S(2)}, u32[]{:S(2)}) async-start(bf16[128,4,1280]{0,2,1:T(8,128)(2,1)} %bitcast.6), calls=%async_computation.2 | async-start | bytes 2621440 | tf_op jit(solution)/shard_map/all_to_all | solution.py:53
  24.7 20.8 %all-to-all-start.1 = ((bf16[128,4,1280]{0,2,1:T(8,128)(2,1)}), bf16[128,4,1280]{0,2,1:T(8,128)(2,1)S(1)}, u32[]{:S(2)}, u32[]{:S(2)}) async-start(bf16[128,4,1280]{0,2,1:T(8,128)(2,1)} %bitcast.212), calls=%async_computation.1 | async-start | bytes 2621440 | tf_op jit(solution)/shard_map/all_to_all | solution.py:52
  45.4 21.6 %all-to-all-start = ((bf16[128,4,1280]{0,2,1:T(8,128)(2,1)}), bf16[128,4,1280]{0,2,1:T(8,128)(2,1)}, u32[]{:S(2)}, u32[]{:S(2)}) async-start(bf16[128,4,1280]{0,2,1:T(8,128)(2,1)} %bitcast.209), calls=%async_computation | async-start | bytes 2621440 | tf_op jit(solution)/shard_map/all_to_all | solution.py:51
  52.6 9.6 %copy-start.16 = (bf16[128,5120]{1,0:T(8,128)(2,1)S(1)}, bf16[128,5120]{1,0:T(8,128)(2,1)}, u32[]{:S(2)}) copy-start(bf16[128,5120]{1,0:T(8,128)(2,1)} %param.8) | copy-start | bytes 3932164
  56.2 174.0 %collective-permute-start = (bf16[2,512,1280]{2,1,0:T(8,128)(2,1)}, bf16[2,512,1280]{2,1,0:T(8,128)(2,1)}, u32[]{:S(2)}, u32[]{:S(2)}) collective-permute-start(bf16[2,512,1280]{2,1,0:T(8,128)(2,1)} %pad_maximum_fusion), channel_id=1, source_target_pairs={{0,4},{4,8},{8,12},{12,16},{16,20},{20,24},{24,28},{1,5},{5,9},{9,... | collective-permute-start | bytes 7864328 | tf_op jit(solution)/shard_map/ppermute | solution.py:20
  67.0 36.2 %all-to-all-start.3 = ((bf16[128,4,1280]{0,2,1:T(8,128)(2,1)}), bf16[128,4,1280]{0,2,1:T(8,128)(2,1)}, u32[]{:S(2)}, u32[]{:S(2)}) async-start(bf16[128,4,1280]{0,2,1:T(8,128)(2,1)} %bitcast.13), calls=%async_computation.3 | async-start | bytes 2621440 | tf_op jit(solution)/shard_map/all_to_all | solution.py:54
  74.0 177.9 %collective-permute-start.1 = (bf16[2,512,1280]{2,1,0:T(8,128)(2,1)}, bf16[2,512,1280]{2,1,0:T(8,128)(2,1)}, u32[]{:S(2)}, u32[]{:S(2)}) collective-permute-start(bf16[2,512,1280]{2,1,0:T(8,128)(2,1)} %pad_maximum_fusion), channel_id=1, source_target_pairs={{4,0},{8,4},{12,8},{16,12},{20,16},{24,20},{28,24},{5,1},{9,5},{13... | collective-permute-start | bytes 7864328 | tf_op jit(solution)/shard_map/ppermute | solution.py:22
  115.1 274.8 %collective-permute-start.2 = (bf16[2,512,1280]{1,2,0:T(8,128)(2,1)}, bf16[2,512,1280]{1,2,0:T(8,128)(2,1)}, u32[]{:S(2)}, u32[]{:S(2)}) collective-permute-start(bf16[2,512,1280]{1,2,0:T(8,128)(2,1)} %constant_dynamic-update-slice_fusion), channel_id=1, source_target_pairs={{0,4},{4,8},{8,12},{12,16},{16,20},{20,24},{24,28},{1,5},{5,9},{9,... | collective-permute-start | bytes 7864328 | tf_op jit(solution)/shard_map/ppermute | solution.py:20
  121.4 281.0 %collective-permute-start.4 = (bf16[2,512,1280]{1,2,0:T(8,128)(2,1)}, bf16[2,512,1280]{1,2,0:T(8,128)(2,1)}, u32[]{:S(2)}, u32[]{:S(2)}) collective-permute-start(bf16[2,512,1280]{1,2,0:T(8,128)(2,1)} %constant_dynamic-update-slice_fusion), channel_id=1, source_target_pairs={{4,0},{8,4},{12,8},{16,12},{20,16},{24,20},{28,24},{5,1},{9,5},{13... | collective-permute-start | bytes 7864328 | tf_op jit(solution)/shard_map/ppermute | solution.py:22
  125.3 11.1 %copy-start.1 = (bf16[512,10,128]{0,2,1:T(8,128)(2,1)}, bf16[512,10,128]{0,2,1:T(8,128)(2,1)S(1)}, u32[]{:S(2)}) copy-start(bf16[512,10,128]{0,2,1:T(8,128)(2,1)S(1)} %reshape_squeeze_stack.6) | copy-start | bytes 3932164
  142.4 137.6 %copy-start.18 = (f32[10,512]{1,0:T(8,128)}, f32[10,512]{1,0:T(8,128)S(1)}, u32[]{:S(2)}) copy-start(f32[10,512]{1,0:T(8,128)S(1)} %get-tuple-element.45) | copy-start | bytes 61444
  263.1 16.9 %copy-start.22 = (f32[10,512]{1,0:T(8,128)}, f32[10,512]{1,0:T(8,128)S(1)}, u32[]{:S(2)}) copy-start(f32[10,512]{1,0:T(8,128)S(1)} %get-tuple-element.43) | copy-start | bytes 61444
  263.1 11.3 %copy-start.10 = (pred[512,512]{0,1:T(8,128)(4,1)S(1)}, pred[512,512]{0,1:T(8,128)(4,1)}, u32[]{:S(2)}) copy-start(pred[512,512]{0,1:T(8,128)(4,1)} %get-tuple-element.40) | copy-start | bytes 786436
  274.4 12.4 %slice-start = ((s8[10485760]{0:T(1024)(128)(4,1)}), s8[4194304]{0:T(1024)(128)(4,1)S(1)}, s32[]{:S(2)}) async-start(s8[10485760]{0:T(1024)(128)(4,1)} %bitcast.186), calls=%async_computation.7 | async-start | bytes 8388608
  274.4 12.4 %slice-start.1 = ((s8[10485760]{0:T(1024)(128)(4,1)}), s8[4194304]{0:T(1024)(128)(4,1)S(1)}, s32[]{:S(2)}) async-start(s8[10485760]{0:T(1024)(128)(4,1)} %bitcast.186), calls=%async_computation.8 | async-start | bytes 8388608
  280.6 9.8 %slice-start.6 = ((s8[10485760]{0:T(1024)(128)(4,1)}), s8[4194304]{0:T(1024)(128)(4,1)S(1)}, s32[]{:S(2)}) async-start(s8[10485760]{0:T(1024)(128)(4,1)} %bitcast.190), calls=%async_computation.13 | async-start | bytes 8388608
  280.6 9.8 %slice-start.7 = ((s8[10485760]{0:T(1024)(128)(4,1)}), s8[4194304]{0:T(1024)(128)(4,1)S(1)}, s32[]{:S(2)}) async-start(s8[10485760]{0:T(1024)(128)(4,1)} %bitcast.190), calls=%async_computation.14 | async-start | bytes 8388608
  328.8 20.0 %slice-start.3 = ((s8[10485760]{0:T(1024)(128)(4,1)}), s8[4194304]{0:T(1024)(128)(4,1)S(1)}, s32[]{:S(2)}) async-start(s8[10485760]{0:T(1024)(128)(4,1)} %bitcast.188), calls=%async_computation.10 | async-start | bytes 8388608
  328.9 16.6 %copy-start.2 = (bf16[512,10,128]{0,2,1:T(8,128)(2,1)S(1)}, bf16[512,10,128]{0,2,1:T(8,128)(2,1)}, u32[]{:S(2)}) copy-start(bf16[512,10,128]{0,2,1:T(8,128)(2,1)} %copy-done.1) | copy-start | bytes 3932164
  328.9 19.9 %slice-start.4 = ((s8[10485760]{0:T(1024)(128)(4,1)}), s8[4194304]{0:T(1024)(128)(4,1)S(1)}, s32[]{:S(2)}) async-start(s8[10485760]{0:T(1024)(128)(4,1)} %bitcast.188), calls=%async_computation.11 | async-start | bytes 8388608
  328.9 19.9 %slice-start.5 = ((s8[10485760]{0:T(1024)(128)(4,1)}), s8[2097152]{0:T(1024)(128)(4,1)S(1)}, s32[]{:S(2)}) async-start(s8[10485760]{0:T(1024)(128)(4,1)} %bitcast.188), calls=%async_computation.12 | async-start | bytes 4194304
  338.2 10.6 %copy-start = (bf16[10,512,512]{1,2,0:T(8,128)(2,1)}, bf16[10,512,512]{1,2,0:T(8,128)(2,1)S(1)}, u32[]{:S(2)}) copy-start(bf16[10,512,512]{1,2,0:T(8,128)(2,1)S(1)} %multiply_convert_fusion.2) | copy-start | bytes 15728644
  338.8 72.1 %collective-permute-start.3 = (f32[2,10,512]{2,1,0:T(8,128)}, f32[2,10,512]{2,1,0:T(8,128)}, u32[]{:S(2)}, u32[]{:S(2)}) collective-permute-start(f32[2,10,512]{2,1,0:T(8,128)} %pad_maximum_fusion.1), channel_id=1, source_target_pairs={{0,4},{4,8},{8,12},{12,16},{16,20},{20,24},{24,28},{1,5},{5,9},{9,... | collective-permute-start | bytes 122888 | tf_op jit(solution)/shard_map/ppermute | solution.py:20
  343.8 79.4 %collective-permute-start.5 = (f32[2,10,512]{2,1,0:T(8,128)}, f32[2,10,512]{2,1,0:T(8,128)}, u32[]{:S(2)}, u32[]{:S(2)}) collective-permute-start(f32[2,10,512]{2,1,0:T(8,128)} %pad_maximum_fusion.1), channel_id=1, source_target_pairs={{4,0},{8,4},{12,8},{16,12},{20,16},{24,20},{28,24},{5,1},{9,5},{13... | collective-permute-start | bytes 122888 | tf_op jit(solution)/shard_map/ppermute | solution.py:22
  348.8 9.7 %copy-start.6 = (bf16[1,512,1280]{1,2,0:T(8,128)(2,1)S(1)}, bf16[1,512,1280]{1,2,0:T(8,128)(2,1)}, u32[]{:S(2)}) copy-start(bf16[1,512,1280]{1,2,0:T(8,128)(2,1)} %copy-done.5) | copy-start | bytes 3932164
  379.7 65.2 %all-to-all-start.4 = ((bf16[4,128,1280]{1,2,0:T(8,128)(2,1)}), bf16[4,128,1280]{1,2,0:T(8,128)(2,1)}, u32[]{:S(2)}, u32[]{:S(2)}) async-start(bf16[4,128,1280]{1,2,0:T(8,128)(2,1)} %copy.336), calls=%async_computation.4 | async-start | bytes 2621440 | tf_op jit(solution)/shard_map/all_to_all | solution.py:133
  384.2 14.2 %slice-start.9 = ((s8[10485760]{0:T(1024)(128)(4,1)}), s8[4194304]{0:T(1024)(128)(4,1)S(1)}, s32[]{:S(2)}) async-start(s8[10485760]{0:T(1024)(128)(4,1)} %bitcast.192), calls=%async_computation.16 | async-start | bytes 8388608
  411.7 12.3 %copy-start.13 = (bf16[512,10,128]{0,2,1:T(8,128)(2,1)S(1)}, bf16[512,10,128]{0,2,1:T(8,128)(2,1)}, u32[]{:S(2)}) copy-start(bf16[512,10,128]{0,2,1:T(8,128)(2,1)} %reshape_squeeze_stack.7) | copy-start | bytes 3932164
  411.7 12.2 %copy-start.30 = (pred[512,512]{0,1:T(8,128)(4,1)S(1)}, pred[512,512]{0,1:T(8,128)(4,1)}, u32[]{:S(2)}) copy-start(pred[512,512]{0,1:T(8,128)(4,1)} %get-tuple-element.36) | copy-start | bytes 786436
  436.5 11.9 %copy-start.14 = (bf16[1,512,1280]{1,2,0:T(8,128)(2,1)S(1)}, bf16[1,512,1280]{1,2,0:T(8,128)(2,1)}, u32[]{:S(2)}) copy-start(bf16[1,512,1280]{1,2,0:T(8,128)(2,1)} %get-tuple-element.20) | copy-start | bytes 3932164
  444.8 20.8 %all-to-all-start.5 = ((bf16[4,128,1280]{1,2,0:T(8,128)(2,1)}), bf16[4,128,1280]{1,2,0:T(8,128)(2,1)S(1)}, u32[]{:S(2)}, u32[]{:S(2)}) async-start(bf16[4,128,1280]{1,2,0:T(8,128)(2,1)} %copy.357), calls=%async_computation.5 | async-start | bytes 2621440 | tf_op jit(solution)/shard_map/all_to_all | solution.py:134
  465.6 20.8 %all-to-all-start.6 = ((bf16[4,128,1280]{1,2,0:T(8,128)(2,1)}), bf16[4,128,1280]{1,2,0:T(8,128)(2,1)S(1)}, u32[]{:S(2)}, u32[]{:S(2)}) async-start(bf16[4,128,1280]{1,2,0:T(8,128)(2,1)} %copy.364), calls=%async_computation.6 | async-start | bytes 2621440 | tf_op jit(solution)/shard_map/all_to_all | solution.py:135
  (26 other events, 123.3 us)
where the time goes:
time: 493 us; the launch traced here: 488 us
  matrix products  140 us (28%)
  waiting for transfers between devices  137 us (28%)
  local copies, waits for them, and re-layouts  125 us (25%)
  starting transfers between devices  49.7 us (10%)
  other arithmetic  34.2 us (7%)
    ppermute x3, waiting for transfers between devices, extended(): lax.ppermute(tail, axis, [(i, (i + 1) % count) for i in range(ends)])  87.8 us
    dot_general x3, matrix products, shards(): jnp.einsum('qhd,khd->hqk', grads_out, value_piece, preferred_element_type...  37.4 us
    dot_general x5, matrix products, masked_scores(): jnp.einsum('qhd,khd->hqk', queries, keys, preferred_element_type=jnp.floa...  28.7 us
    dot_general x3, matrix products, key_terms(): jnp.einsum('hqk,qhd->khd', dscore, queries, preferred_element_type=jnp.fl...  26.4 us
    dot_general x3, matrix products, shards(): jnp.einsum('hqk,khd->qhd', dscore, key_piece, preferred_element_type=jnp....  25.6 us
    dot_general x3, matrix products, key_terms(): jnp.einsum('hqk,qhd->khd', probs_b, grads_out, preferred_element_type=jnp...  21.8 us
    ppermute x3, starting transfers between devices, extended(): lax.ppermute(tail, axis, [(i, (i + 1) % count) for i in range(ends)])  17 us
    all_to_all x1, waiting for transfers between devices, shards(): lax.all_to_all(value_in, 'tp', split_axis=1, concat_axis=0, tiled=True)  15.8 us
  transfers between devices with their start and end apart: 13, of which 6 were waited for; matrix products, arithmetic and copies ran while one was open for 61% of the time, Pallas kernels for 0%

commit v1 on v0

v1 whole, which is shorter than its diff:
```python
import functools

import jax
import jax.numpy as jnp
import numpy as np
from jax import lax
from jax.experimental import pallas as pl
from jax.experimental.pallas import tpu as pltpu
from jax.sharding import Mesh
from jax.sharding import PartitionSpec as P

HEAD_DIM = 128
NEG = -1e30
FLOOR = -1e29
UNIT = 128
TILE = 256
WIDTHS = (2, 3, 4, 5, 6, 8, 10)


def pack_kernel(*refs):
    ins, out = refs[:-1], refs[-1]
    for number, ref in enumerate(ins):
        out[0, number] = ref[...]


def pack(arrays, peers, first, count):
    rows, width = arrays[0].shape
    each = width // peers
    spec = pl.BlockSpec(
        (pl.Element(rows), pl.Element(count)), lambda d: (0, pl.multiple_of(d * each + first, 128))
    )
    return pl.pallas_call(
        pack_kernel,
        grid=(peers,),
        in_specs=[spec] * len(arrays),
        out_specs=pl.BlockSpec((1, len(arrays), rows, count), lambda d: (d, 0, 0, 0)),
        out_shape=jax.ShapeDtypeStruct((peers, len(arrays), rows, count), arrays[0].dtype),
        name="pack",
    )(*arrays)


def unpack_kernel(spans, kinds, *refs):
    ins, outs = refs[: len(spans)], refs[len(spans) :]
    for (first, count), ref in zip(spans, ins):
        for kind in range(kinds):
            outs[kind][:, first : first + count] = ref[0, kind]


def unpack(blocks, spans):
    peers, kinds, rows, _ = blocks[0].shape
    each = sum(count for _, count in spans)
    return pl.pallas_call(
        functools.partial(unpack_kernel, spans, kinds),
        grid=(peers,),
        in_specs=[
            pl.BlockSpec((1, kinds, rows, count), lambda d: (d, 0, 0, 0)) for _, count in spans
        ],
        out_specs=[pl.BlockSpec((rows, each), lambda d: (0, d))] * kinds,
        out_shape=[jax.ShapeDtypeStruct((rows, peers * each), blocks[0].dtype)] * kinds,
        name="unpack",
    )(*blocks)


def attention_kernel(
    widths,
    half,
    meta,
    seg_key,
    seg_query,
    left,
    own,
    right,
    out_left,
    out_own,
    out_right,
    qw,
    kw,
    vw,
    gw,
    kt,
    dq,
    dk,
    dv,
):
    window = qw.shape[0]
    scale = HEAD_DIM ** (-0.5)
    factor = scale * float(np.log2(np.e))
    group = window - 2 * half
    parts = ((left, 0, half), (own, half, group), (right, half + group, half))
    for number, target in enumerate((qw, kw, vw, gw)):
        for source, first, count in parts:
            target[first : first + count] = source[:, number].reshape(count, HEAD_DIM)
    for tile in range(window // TILE):
        kt[:, tile * TILE : (tile + 1) * TILE] = kw[tile * TILE : (tile + 1) * TILE].T
    dq[...] = jnp.zeros_like(dq)
    dk[...] = jnp.zeros_like(dk)
    dv[...] = jnp.zeros_like(dv)

    def visit(tile, width):
        rows = pl.ds(pl.multiple_of(tile * TILE, TILE), TILE)
        keys = pl.ds(pl.multiple_of(meta[0, tile] * UNIT, UNIT), width * UNIT)
        q, g, k, v = qw[rows], gw[rows], kw[keys], vw[keys]
        over = (((1,), (1,)), ((), ()))
        scores = lax.dot_general(k, q, over, preferred_element_type=jnp.float32)
        dprob = lax.dot_general(v, g, over, preferred_element_type=jnp.float32)
        marks = jnp.concatenate([seg_key[keys]] * (TILE // 128), axis=1)
        scores = jnp.where(marks == seg_query[:, rows], scores, NEG)
        top = jnp.maximum(jnp.max(scores, axis=0, keepdims=True), FLOOR)
        raised = jnp.exp2((scores - top) * factor)
        total = jnp.sum(raised, axis=0, keepdims=True)
        inverse = jnp.where(total > 0.0, 1.0 / total, 0.0)
        dot = jnp.sum(raised * dprob, axis=0, keepdims=True) * inverse
        probs = raised * inverse
        probs_b = probs.astype(jnp.bfloat16)
        dscore = (probs * (dprob - dot)).astype(jnp.bfloat16)
        dv[keys] += jnp.dot(probs_b, g, preferred_element_type=jnp.float32)
        dk[keys] += jnp.dot(dscore, q, preferred_element_type=jnp.float32)
        turned = jnp.dot(kt[:, keys], dscore, preferred_element_type=jnp.float32)
        dq[rows] = turned.T * scale

    def step(tile, carry):
        for width in widths:
            pl.when(meta[1, tile] == width)(functools.partial(visit, tile, width))
        return carry

    lax.fori_loop(0, window // TILE, step, 0)
    for target, first, count in (
        (out_left, 0, half),
        (out_own, half, group),
        (out_right, half + group, half),
    ):
        shape = (target.shape[0],) + target.shape[2:]
        span = slice(first, first + count)
        target[:, 0] = dq[span].astype(jnp.bfloat16).reshape(shape)
        target[:, 1] = (dk[span] * scale).astype(jnp.bfloat16).reshape(shape)
        target[:, 2] = dv[span].astype(jnp.bfloat16).reshape(shape)


def attention(meta, seg_key, seg_query, left, own, right, widths):
    peers, kinds, rows, width = own.shape
    edge = left.shape[0]
    half = edge * rows
    window = peers * rows + 2 * half

    def block(count, number):
        return pl.BlockSpec((count, number, rows, HEAD_DIM), lambda h, _: (0, 0, 0, h))

    def shape(count):
        return jax.ShapeDtypeStruct((count, 3, rows, width), jnp.bfloat16)

    elements = width // HEAD_DIM * window * 5 * UNIT
    return pl.pallas_call(
        functools.partial(attention_kernel, widths, half),
        grid_spec=pltpu.PrefetchScalarGridSpec(
            num_scalar_prefetch=1,
            grid=(width // HEAD_DIM,),
            in_specs=[
                pl.BlockSpec((window, 128), lambda h, _: (0, 0)),
                pl.BlockSpec((1, window), lambda h, _: (0, 0)),
                block(edge, 4),
                block(peers, 4),
                block(edge, 4),
            ],
            out_specs=[block(edge, 3), block(peers, 3), block(edge, 3)],
            scratch_shapes=[pltpu.VMEM((window, HEAD_DIM), jnp.bfloat16)] * 4
            + [pltpu.VMEM((HEAD_DIM, window), jnp.bfloat16)]
            + [pltpu.VMEM((window, HEAD_DIM), jnp.float32)] * 3,
        ),
        out_shape=[shape(edge), shape(peers), shape(edge)],
        cost_estimate=pl.CostEstimate(
            flops=elements * 10 * HEAD_DIM,
            transcendentals=elements,
            bytes_accessed=own.size * 4 + left.size * 8,
        ),
        name="attention",
    )(meta, seg_key, seg_query, left, own, right)


def plan(lengths, me, group, half, tokens, widths):
    window = group + 2 * half
    count = lengths.shape[0]
    order = jnp.arange(count, dtype=jnp.int32)
    ends = jnp.sum(jnp.where(order[:, None] <= order[None, :], lengths[:, None], 0), axis=0)
    base = me * group - half
    at = base + jnp.arange(window, dtype=jnp.int32)
    passed = ends[:, None] <= at[None, :]
    seg = jnp.sum(passed.astype(jnp.int32), axis=0)
    start = jnp.sum(jnp.where(passed, lengths[:, None], 0), axis=0)
    end = jnp.min(jnp.where(passed, tokens, ends[:, None]), axis=0)
    low, high = start // group, (end - 1) // group
    edge = high * group
    owner = jnp.where((low == high) | (edge - start >= end - edge), low, high)
    valid = (owner == me) & (at >= 0) & (at < tokens)
    seg_key = jnp.broadcast_to(jnp.where(valid, seg, -1)[:, None], (window, 128))
    seg_query = jnp.where(valid, seg, -2)[None, :]
    first = jnp.min(jnp.where(valid, start - base, window).reshape(-1, TILE), axis=1) // UNIT
    last = jnp.max(jnp.where(valid, end - base, 0).reshape(-1, TILE), axis=1)
    need = (last + UNIT - 1) // UNIT - first
    chosen = jnp.full_like(need, widths[-1])
    for width in reversed(widths):
        chosen = jnp.where(need <= width, width, chosen)
    chosen = jnp.where(last > 0, chosen, 0)
    first = jnp.clip(first, 0, window // UNIT - chosen)
    return jnp.stack([first, chosen]).astype(jnp.int32), seg_key, seg_query


def shards(query, key_in, value_in, out_grad, lengths):
    arrays = (query, key_in, value_in, out_grad)
    plane = ("r", "tp")
    groups = lax.axis_size("g")
    peers = lax.axis_size("r") * lax.axis_size("tp")
    rows, width = query.shape
    each = width // peers
    group = rows * peers
    half = rows * lax.axis_size("tp") // 2
    edge = half // rows
    window = group + 2 * half
    tokens = group * groups
    widths = tuple(w for w in WIDTHS if w < window // UNIT and w <= 10)
    if window // UNIT <= 10:
        widths = widths + (window // UNIT,)
    meta, seg_key, seg_query = plan(lengths, lax.axis_index("g"), group, half, tokens, widths)
    up = [(i, i + 1) for i in range(groups - 1)]
    down = [(i + 1, i) for i in range(groups - 1)]
    heads = each // HEAD_DIM
    counts = (heads - heads // 2, heads // 2)
    spans, first = [], 0
    for count in counts:
        if count:
            spans.append((first * HEAD_DIM, count * HEAD_DIM))
            first += count
    gathered = []
    for first, count in spans:
        packed = pack(arrays, peers, first, count)
        own = lax.all_to_all(packed, plane, split_axis=0, concat_axis=0, tiled=True)
        gathered.append(own)
    returned = []
    for own in gathered:
        left = lax.ppermute(own[peers - edge :], "g", up)
        right = lax.ppermute(own[:edge], "g", down)
        out_left, out_own, out_right = attention(
            meta, seg_key, seg_query, left, own, right, widths
        )
        from_right = lax.ppermute(out_left, "g", down)
        from_left = lax.ppermute(out_right, "g", up)
        out_own = out_own.at[:edge].add(from_left)
        out_own = out_own.at[peers - edge :].add(from_right)
        returned.append(
            lax.all_to_all(out_own, plane, split_axis=0, concat_axis=0, tiled=True)
        )
    return tuple(unpack(returned, spans))


def solution(mesh):
    ctx, tp = mesh.devices.shape
    heads_of = lambda width: width // HEAD_DIM

    def run(query, key_in, value_in, out_grad, lengths):
        heads = heads_of(query.shape[1])
        near = max(r for r in range(1, ctx + 1) if ctx % r == 0 and heads % (r * tp) == 0)
        finer = Mesh(mesh.devices.reshape(ctx // near, near, tp), ("g", "r", "tp"))
        placed = P(("g", "r", "tp"), None)
        return jax.shard_map(
            shards,
            mesh=finer,
            in_specs=(placed,) * 4 + (P(),),
            out_specs=(placed,) * 3,
            check_vma=False,
        )(query, key_in, value_in, out_grad, lengths)

    return run
```

time: 493 us -> 212 us (0.43); the launches traced: 488 us -> 212 us
  matrix products: 140 us -> 0 us
  local copies, waits for them, and re-layouts: 125 us -> 8.52 us
  waiting for transfers between devices: 137 us -> 70.5 us
  Pallas kernels: 0 us -> 46.5 us
  blocking collectives: 0 us -> 33.2 us
  other arithmetic: 34.2 us -> 9.46 us
  starting transfers between devices: 49.7 us -> 42.9 us
    dot_general x17 -> x0, matrix products: 140 us -> none  [the longest x3 37.4 us: shards(): jnp.einsum('qhd,khd->hqk', grads_out, value_piece, preferred_element_type...]
    pallas_call x0 -> x5, Pallas kernels: none -> 46.5 us  [the longest x2 28.1 us: attention(): pl.pallas_call(functools.partial(attention_kernel, widths, half), grid_sp...]
    ppermute x6 -> x8, waiting for transfers between devices: 87.8 us -> 51.1 us  [the longest x2 23.5 us: shards(): from_right = lax.ppermute(out_left, 'g', down)]
    all_to_all x0 -> x1, blocking collectives: none -> 33.2 us  [shards(): lax.all_to_all(out_own, plane, split_axis=0, concat_axis=0, tiled=True)]
    all_to_all x6 -> x0, local copies, waits for them, and re-layouts: 30.4 us -> none  [the longest x2 8.79 us: shards(): lax.all_to_all(key_in, 'tp', split_axis=1, concat_axis=0, tiled=True)]
    all_to_all x7 -> x3, waiting for transfers between devices: 49.5 us -> 19.4 us  [the longest x2 19.4 us: shards(): own = lax.all_to_all(packed, plane, split_axis=0, concat_axis=0, tiled=True)]
    slice x9 -> x2, local copies, waits for them, and re-layouts: 21.1 us -> 2.6 us  [shards(): right = lax.ppermute(own[:edge], 'g', down)]
    convert_element_type x9 -> x0, local copies, waits for them, and re-layouts: 17.1 us -> none  [the longest x3 8.52 us: shards(): query_grad = (query_sum * scale).reshape(rows, width).astype(jnp.bfloat16)]
  transfers between devices with their start and end apart: 13 -> 11, of which waited for: 6 -> 7; matrix products, arithmetic and copies ran while one was open for 61% -> 6% of each run, Pallas kernels for 0% -> 16%
where the time goes in v1:
time: 212 us
  waiting for transfers between devices  70.5 us (33%)
  Pallas kernels  46.5 us (22%)
  starting transfers between devices  42.9 us (20%)
  blocking collectives  33.2 us (16%)
  other arithmetic  9.46 us (4%)
  local copies, waits for them, and re-layouts  8.52 us (4%)
    all_to_all x1, blocking collectives, shards(): lax.all_to_all(out_own, plane, split_axis=0, concat_axis=0, tiled=True)  33.2 us
    pallas_call x2, Pallas kernels, attention(): pl.pallas_call(functools.partial(attention_kernel, widths, half), grid_sp...  28.1 us
    ppermute x2, waiting for transfers between devices, shards(): from_right = lax.ppermute(out_left, 'g', down)  23.5 us
    ppermute x2, starting transfers between devices, shards(): from_left = lax.ppermute(out_right, 'g', up)  19.7 us
    all_to_all x2, waiting for transfers between devices, shards(): own = lax.all_to_all(packed, plane, split_axis=0, concat_axis=0, tiled=True)  19.4 us
    ppermute x2, waiting for transfers between devices, shards(): from_left = lax.ppermute(out_right, 'g', up)  15.1 us
    pallas_call x2, Pallas kernels, pack(): pl.pallas_call(pack_kernel, grid=(peers,), in_specs=[spec] * len(arrays),...  12 us
    ppermute x2, waiting for transfers between devices, shards(): left = lax.ppermute(own[peers - edge:], 'g', up)  9.13 us
  transfers between devices with their start and end apart: 11, of which 7 were waited for; matrix products, arithmetic and copies ran while one was open for 6% of the time, Pallas kernels for 16%

profile of v1, /device:TPU:0, one launch (start us, length us, event | category | flops | bytes accessed | tf_op | source)
XLA Modules:
  0.0 212.0 jit_solution(3772705725660953691)
XLA Ops:
  0.6 5.7 %pack.3 = bf16[8,4,128,256]{3,2,1,0:T(8,128)(2,1)} custom-call(bf16[128,5120]{1,0:T(8,128)(2,1)} %refs_0_.3, bf16[128,5120]{1,0:T(8,128)(2,1)} %refs_1_.3, bf16[128,5120]{1,0:T(8,128)(2,1)} %refs_2_.3, bf16[128,5120]{1,0:T(8,128)(2,1)} %refs_3_.3), custom_call_target="tpu_custom_call" | custom-call | tf_op jit(solution)/shard_map/pack/pallas_call | solution.py:32
  6.3 5.2 %all-to-all-start.2 = ((bf16[8,4,128,256]{3,2,1,0:T(8,128)(2,1)}), bf16[8,4,128,256]{3,2,1,0:T(8,128)(2,1)S(1)}, u32[]{:S(2)}, u32[]{:S(2)}) async-start(bf16[8,4,128,256]{3,2,1,0:T(8,128)(2,1)} %pack.3), calls=%async_computation.2 | async-start | bytes 4194304 | tf_op jit(solution)/shard_map/all_to_all | solution.py:235
  11.5 6.3 %pack.2 = bf16[8,4,128,384]{3,2,1,0:T(8,128)(2,1)} custom-call(bf16[128,5120]{1,0:T(8,128)(2,1)} %refs_0_.3, bf16[128,5120]{1,0:T(8,128)(2,1)} %refs_1_.3, bf16[128,5120]{1,0:T(8,128)(2,1)} %refs_2_.3, bf16[128,5120]{1,0:T(8,128)(2,1)} %refs_3_.3), custom_call_target="tpu_custom_call" | custom-call | tf_op jit(solution)/shard_map/pack/pallas_call | solution.py:32
  17.8 19.4 %all-to-all-done.2.own = bf16[8,4,128,256]{3,2,1,0:T(8,128)(2,1)S(1)} async-done(((bf16[8,4,128,256]{3,2,1,0:T(8,128)(2,1)}), bf16[8,4,128,256]{3,2,1,0:T(8,128)(2,1)S(1)}, u32[]{:S(2)}, u32[]{:S(2)}) %all-to-all-start.2) | async-done | bytes 2097184 | tf_op jit(solution)/shard_map/all_to_all | solution.py:235
  37.2 1.4 copy-done.2
  38.6 3.6 %all-to-all-start = ((bf16[8,4,128,384]{3,2,1,0:T(8,128)(2,1)}), bf16[8,4,128,384]{3,2,1,0:T(8,128)(2,1)S(1)}, u32[]{:S(2)}, u32[]{:S(2)}) async-start(bf16[8,4,128,384]{3,2,1,0:T(8,128)(2,1)} %pack.2), calls=%async_computation | async-start | bytes 6291456 | tf_op jit(solution)/shard_map/all_to_all | solution.py:235
  42.7 1.3 fusion.20
  44.0 3.5 %collective-permute-start.4 = (bf16[2,4,128,256]{3,2,1,0:T(8,128)(2,1)S(1)}, bf16[2,4,128,256]{3,2,1,0:T(8,128)(2,1)S(1)}, u32[]{:S(2)}, u32[]{:S(2)}) collective-permute-start(bf16[2,4,128,256]{3,2,1,0:T(8,128)(2,1)S(1)} %get-tuple-element.71), channel_id=1, source_target_pairs={{0,8},{8,16},{16,24},{1,9},{9,17},{17,25},{2,10},{10,18},{18,26},{... | collective-permute-start | bytes 1572872 | tf_op jit(solution)/shard_map/ppermute | solution.py:239
  47.5 1.3 collective-permute-start.5
  50.1 9.1 %collective-permute-done.4.left = bf16[2,4,128,256]{3,2,1,0:T(8,128)(2,1)S(1)} collective-permute-done((bf16[2,4,128,256]{3,2,1,0:T(8,128)(2,1)S(1)}, bf16[2,4,128,256]{3,2,1,0:T(8,128)(2,1)S(1)}, u32[]{:S(2)}, u32[]{:S(2)}) %collective-permute-start.4) | collective-permute-done | bytes 524320 | tf_op jit(solution)/shard_map/ppermute | solution.py:239
  60.0 3.5 %collective-permute-done.5.right = bf16[2,4,128,256]{3,2,1,0:T(8,128)(2,1)} collective-permute-done((bf16[2,4,128,256]{3,2,1,0:T(8,128)(2,1)S(1)}, bf16[2,4,128,256]{3,2,1,0:T(8,128)(2,1)}, u32[]{:S(2)}, u32[]{:S(2)}) %collective-permute-start.5) | collective-permute-done | bytes 524320 | tf_op jit(solution)/shard_map/ppermute | solution.py:240
  63.5 1.1 broadcast_in_dim.73.seg_key
  64.6 12.0 %attention.3 = (bf16[2,3,128,256]{3,2,1,0:T(8,128)(2,1)}, bf16[8,3,128,256]{3,2,1,0:T(8,128)(2,1)}, bf16[2,3,128,256]{3,2,1,0:T(8,128)(2,1)}) custom-call(s32[2,6]{1,0:T(2,128)} %pad_add_fusion.meta, s32[1536,128]{1,0:T(8,128)} %broadcast_in_dim.73.seg_key, s32[1,1536]{1,0:T(1,128)} %and_select_fusion.seg_query, bf16[2,4,128,256]{3,2,1,0:T(8,128)(2,1)} %copy-done.6, ...), custom_call_target="tpu_custom_call" | custom-call | flops 2516582400 | bytes 6291456 | tf_op jit(solution)/shard_map/attention/pallas_call | solution.py:152
  76.6 9.1 %collective-permute-start.6 = (bf16[2,3,128,256]{3,2,1,0:T(8,128)(2,1)}, bf16[2,3,128,256]{3,2,1,0:T(8,128)(2,1)S(1)}, u32[]{:S(2)}, u32[]{:S(2)}) collective-permute-start(bf16[2,3,128,256]{3,2,1,0:T(8,128)(2,1)} %get-tuple-element.61), channel_id=1, source_target_pairs={{0,8},{8,16},{16,24},{1,9},{9,17},{17,25},{2,10},{10,18},{18,26},{... | collective-permute-start | bytes 1179656 | tf_op jit(solution)/shard_map/ppermute | solution.py:245
  85.7 1.3 fusion.19
  87.9 1.9 collective-permute-start
  89.8 1.3 collective-permute-start.1
  91.1 1.3 collective-permute-start.7
  92.4 3.0 %collective-permute-done.6 = bf16[2,3,128,256]{3,2,1,0:T(8,128)(2,1)S(1)} collective-permute-done((bf16[2,3,128,256]{3,2,1,0:T(8,128)(2,1)}, bf16[2,3,128,256]{3,2,1,0:T(8,128)(2,1)S(1)}, u32[]{:S(2)}, u32[]{:S(2)}) %collective-permute-start.6) | collective-permute-done | bytes 393248 | tf_op jit(solution)/shard_map/ppermute | solution.py:245
  95.5 1.8 add_dynamic-update-slice_fusion.1
  97.3 21.5 %collective-permute-done.7 = bf16[2,3,128,256]{3,2,1,0:T(8,128)(2,1)S(1)} collective-permute-done((bf16[2,3,128,256]{3,2,1,0:T(8,128)(2,1)S(1)}, bf16[2,3,128,256]{3,2,1,0:T(8,128)(2,1)S(1)}, u32[]{:S(2)}, u32[]{:S(2)}) %collective-permute-start.7) | collective-permute-done | bytes 393248 | tf_op jit(solution)/shard_map/ppermute | solution.py:244
  118.8 1.9 fusion.1
  120.6 3.8 %all-to-all-start.3 = ((bf16[8,3,128,256]{3,2,1,0:T(8,128)(2,1)}), bf16[8,3,128,256]{3,2,1,0:T(8,128)(2,1)S(1)}, u32[]{:S(2)}, u32[]{:S(2)}) async-start(bf16[8,3,128,256]{3,2,1,0:T(8,128)(2,1)} %fusion.1), calls=%async_computation.3 | async-start | bytes 3145728 | tf_op jit(solution)/shard_map/all_to_all | solution.py:249
  126.2 16.1 %attention.2 = (bf16[2,3,128,384]{3,2,1,0:T(8,128)(2,1)}, bf16[8,3,128,384]{3,2,1,0:T(8,128)(2,1)}, bf16[2,3,128,384]{3,2,1,0:T(8,128)(2,1)}) custom-call(s32[2,6]{1,0:T(2,128)} %pad_add_fusion.meta, s32[1536,128]{1,0:T(8,128)} %broadcast_in_dim.73.seg_key, s32[1,1536]{1,0:T(1,128)} %and_select_fusion.seg_query, bf16[2,4,128,384]{3,2,1,0:T(8,128)(2,1)} %copy-done.4, ...), custom_call_target="tpu_custom_call" | custom-call | flops 3774873600 | bytes 9437184 | tf_op jit(solution)/shard_map/attention/pallas_call | solution.py:152
  142.3 10.6 %collective-permute-start.2 = (bf16[2,3,128,384]{3,2,1,0:T(8,128)(2,1)}, bf16[2,3,128,384]{3,2,1,0:T(8,128)(2,1)S(1)}, u32[]{:S(2)}, u32[]{:S(2)}) collective-permute-start(bf16[2,3,128,384]{3,2,1,0:T(8,128)(2,1)} %get-tuple-element.58), channel_id=1, source_target_pairs={{0,8},{8,16},{16,24},{1,9},{9,17},{17,25},{2,10},{10,18},{18,26},{... | collective-permute-start | bytes 1769480 | tf_op jit(solution)/shard_map/ppermute | solution.py:245
  152.9 1.3 collective-permute-start.3
  154.2 12.0 %collective-permute-done.2 = bf16[2,3,128,384]{3,2,1,0:T(8,128)(2,1)S(1)} collective-permute-done((bf16[2,3,128,384]{3,2,1,0:T(8,128)(2,1)}, bf16[2,3,128,384]{3,2,1,0:T(8,128)(2,1)S(1)}, u32[]{:S(2)}, u32[]{:S(2)}) %collective-permute-start.2) | collective-permute-done | bytes 589856 | tf_op jit(solution)/shard_map/ppermute | solution.py:245
  166.3 2.0 add_dynamic-update-slice_fusion
  168.3 2.0 collective-permute-done.3
  170.3 2.0 fusion
  172.3 33.2 %all_to_all.20.refs_0_ = bf16[8,3,128,384]{3,2,1,0:T(8,128)(2,1)} all-to-all(bf16[8,3,128,384]{3,2,1,0:T(8,128)(2,1)} %fusion), channel_id=1, replica_groups=mesh['g'=4,'r'=2,'tp'=4] {'r','tp'}, dimensions={0} | all-to-all | bytes 4718592 | tf_op jit(solution)/shard_map/all_to_all | solution.py:249
  205.5 6.4 %unpack.1 = (bf16[128,5120]{1,0:T(8,128)(2,1)}, bf16[128,5120]{1,0:T(8,128)(2,1)}, bf16[128,5120]{1,0:T(8,128)(2,1)}) custom-call(bf16[8,3,128,384]{3,2,1,0:T(8,128)(2,1)} %all_to_all.20.refs_0_, bf16[8,3,128,256]{3,2,1,0:T(8,128)(2,1)} %copy-done.1), custom_call_target="tpu_custom_call" | custom-call | tf_op jit(solution)/shard_map/unpack/pallas_call | solution.py:52
  (29 shorter events, 5.1 us)
Async XLA Ops:
  6.3 30.9 %all-to-all-start.2 = ((bf16[8,4,128,256]{3,2,1,0:T(8,128)(2,1)}), bf16[8,4,128,256]{3,2,1,0:T(8,128)(2,1)S(1)}, u32[]{:S(2)}, u32[]{:S(2)}) async-start(bf16[8,4,128,256]{3,2,1,0:T(8,128)(2,1)} %pack.3), calls=%async_computation.2 | async-start | bytes 4194304 | tf_op jit(solution)/shard_map/all_to_all | solution.py:235
  17.8 24.4 %copy-start.3 = (s32[32]{0:T(128)S(1)}, s32[32]{0:T(128)}, u32[]{:S(2)}) copy-start(s32[32]{0:T(128)} %param.17) | copy-start | bytes 388
  37.2 1.4 copy-start.2
  38.6 47.1 %all-to-all-start = ((bf16[8,4,128,384]{3,2,1,0:T(8,128)(2,1)}), bf16[8,4,128,384]{3,2,1,0:T(8,128)(2,1)S(1)}, u32[]{:S(2)}, u32[]{:S(2)}) async-start(bf16[8,4,128,384]{3,2,1,0:T(8,128)(2,1)} %pack.2), calls=%async_computation | async-start | bytes 6291456 | tf_op jit(solution)/shard_map/all_to_all | solution.py:235
  44.0 15.2 %collective-permute-start.4 = (bf16[2,4,128,256]{3,2,1,0:T(8,128)(2,1)S(1)}, bf16[2,4,128,256]{3,2,1,0:T(8,128)(2,1)S(1)}, u32[]{:S(2)}, u32[]{:S(2)}) collective-permute-start(bf16[2,4,128,256]{3,2,1,0:T(8,128)(2,1)S(1)} %get-tuple-element.71), channel_id=1, source_target_pairs={{0,8},{8,16},{16,24},{1,9},{9,17},{17,25},{2,10},{10,18},{18,26},{... | collective-permute-start | bytes 1572872 | tf_op jit(solution)/shard_map/ppermute | solution.py:239
  47.5 15.9 %collective-permute-start.5 = (bf16[2,4,128,256]{3,2,1,0:T(8,128)(2,1)S(1)}, bf16[2,4,128,256]{3,2,1,0:T(8,128)(2,1)}, u32[]{:S(2)}, u32[]{:S(2)}) collective-permute-start(bf16[2,4,128,256]{3,2,1,0:T(8,128)(2,1)S(1)} %get-tuple-element.70), channel_id=1, source_target_pairs={{8,0},{16,8},{24,16},{9,1},{17,9},{25,17},{10,2},{18,10},{26,18},{... | collective-permute-start | bytes 1572872 | tf_op jit(solution)/shard_map/ppermute | solution.py:240
  59.2 0.8 copy-start.6
  76.6 18.9 %collective-permute-start.6 = (bf16[2,3,128,256]{3,2,1,0:T(8,128)(2,1)}, bf16[2,3,128,256]{3,2,1,0:T(8,128)(2,1)S(1)}, u32[]{:S(2)}, u32[]{:S(2)}) collective-permute-start(bf16[2,3,128,256]{3,2,1,0:T(8,128)(2,1)} %get-tuple-element.61), channel_id=1, source_target_pairs={{0,8},{8,16},{16,24},{1,9},{9,17},{17,25},{2,10},{10,18},{18,26},{... | collective-permute-start | bytes 1179656 | tf_op jit(solution)/shard_map/ppermute | solution.py:245
  85.7 2.2 %copy-start = (bf16[8,4,128,384]{3,2,1,0:T(8,128)(2,1)}, bf16[8,4,128,384]{3,2,1,0:T(8,128)(2,1)S(1)}, u32[]{:S(2)}) copy-start(bf16[8,4,128,384]{3,2,1,0:T(8,128)(2,1)S(1)} %all-to-all-done.own) | copy-start | bytes 9437188
  85.7 5.4 %copy-start.7 = (bf16[2,3,128,256]{3,2,1,0:T(8,128)(2,1)S(1)}, bf16[2,3,128,256]{3,2,1,0:T(8,128)(2,1)}, u32[]{:S(2)}) copy-start(bf16[2,3,128,256]{3,2,1,0:T(8,128)(2,1)} %get-tuple-element.62) | copy-start | bytes 1179652
  87.9 36.5 %collective-permute-start = (bf16[2,4,128,384]{3,2,1,0:T(8,128)(2,1)}, bf16[2,4,128,384]{3,2,1,0:T(8,128)(2,1)S(1)}, u32[]{:S(2)}, u32[]{:S(2)}) collective-permute-start(bf16[2,4,128,384]{3,2,1,0:T(8,128)(2,1)} %get-tuple-element.69), channel_id=1, source_target_pairs={{0,8},{8,16},{16,24},{1,9},{9,17},{17,25},{2,10},{10,18},{18,26},{... | collective-permute-start | bytes 2359304 | tf_op jit(solution)/shard_map/ppermute | solution.py:239
  89.8 34.6 %collective-permute-start.1 = (bf16[2,4,128,384]{3,2,1,0:T(8,128)(2,1)}, bf16[2,4,128,384]{3,2,1,0:T(8,128)(2,1)S(1)}, u32[]{:S(2)}, u32[]{:S(2)}) collective-permute-start(bf16[2,4,128,384]{3,2,1,0:T(8,128)(2,1)} %get-tuple-element.68), channel_id=1, source_target_pairs={{8,0},{16,8},{24,16},{9,1},{17,9},{25,17},{10,2},{18,10},{26,18},{... | collective-permute-start | bytes 2359304 | tf_op jit(solution)/shard_map/ppermute | solution.py:240
  91.1 27.6 %collective-permute-start.7 = (bf16[2,3,128,256]{3,2,1,0:T(8,128)(2,1)S(1)}, bf16[2,3,128,256]{3,2,1,0:T(8,128)(2,1)S(1)}, u32[]{:S(2)}, u32[]{:S(2)}) collective-permute-start(bf16[2,3,128,256]{3,2,1,0:T(8,128)(2,1)S(1)} %copy-done.7), channel_id=1, source_target_pairs={{8,0},{16,8},{24,16},{9,1},{17,9},{25,17},{10,2},{18,10},{26,18},{... | collective-permute-start | bytes 1179656 | tf_op jit(solution)/shard_map/ppermute | solution.py:244
  120.6 51.7 %all-to-all-start.3 = ((bf16[8,3,128,256]{3,2,1,0:T(8,128)(2,1)}), bf16[8,3,128,256]{3,2,1,0:T(8,128)(2,1)S(1)}, u32[]{:S(2)}, u32[]{:S(2)}) async-start(bf16[8,3,128,256]{3,2,1,0:T(8,128)(2,1)} %fusion.1), calls=%async_computation.3 | async-start | bytes 3145728 | tf_op jit(solution)/shard_map/all_to_all | solution.py:249
  124.4 0.9 copy-start.4
  125.3 0.9 copy-start.5
  142.3 23.9 %collective-permute-start.2 = (bf16[2,3,128,384]{3,2,1,0:T(8,128)(2,1)}, bf16[2,3,128,384]{3,2,1,0:T(8,128)(2,1)S(1)}, u32[]{:S(2)}, u32[]{:S(2)}) collective-permute-start(bf16[2,3,128,384]{3,2,1,0:T(8,128)(2,1)} %get-tuple-element.58), channel_id=1, source_target_pairs={{0,8},{8,16},{16,24},{1,9},{9,17},{17,25},{2,10},{10,18},{18,26},{... | collective-permute-start | bytes 1769480 | tf_op jit(solution)/shard_map/ppermute | solution.py:245
  152.9 17.4 %collective-permute-start.3 = (bf16[2,3,128,384]{3,2,1,0:T(8,128)(2,1)}, bf16[2,3,128,384]{3,2,1,0:T(8,128)(2,1)S(1)}, u32[]{:S(2)}, u32[]{:S(2)}) collective-permute-start(bf16[2,3,128,384]{3,2,1,0:T(8,128)(2,1)} %get-tuple-element.59), channel_id=1, source_target_pairs={{8,0},{16,8},{24,16},{9,1},{17,9},{25,17},{10,2},{18,10},{26,18},{... | collective-permute-start | bytes 1769480 | tf_op jit(solution)/shard_map/ppermute | solution.py:244
  172.3 33.2 %copy-start.1 = (bf16[8,3,128,256]{3,2,1,0:T(8,128)(2,1)}, bf16[8,3,128,256]{3,2,1,0:T(8,128)(2,1)S(1)}, u32[]{:S(2)}) copy-start(bf16[8,3,128,256]{3,2,1,0:T(8,128)(2,1)S(1)} %all-to-all-done.3.refs_1_) | copy-start | bytes 4718596

commit v2 on v1

v2 whole, which is shorter than its diff:
```python
import functools

import jax
import jax.numpy as jnp
import numpy as np
from jax import lax
from jax.experimental import pallas as pl
from jax.experimental.pallas import tpu as pltpu
from jax.sharding import Mesh
from jax.sharding import PartitionSpec as P

HEAD_DIM = 128
NEG = -1e30
FLOOR = -1e29
UNIT = 128
CHUNK = 2
TILE = 256
WIDTHS = (4, 5, 6, 8, 10)


def copy_all(pairs, sems):
    copies = [
        pltpu.make_async_copy(source, target, sems.at[number])
        for number, (source, target) in enumerate(pairs)
    ]
    for copy in copies:
        copy.start()
    for copy in copies:
        copy.wait()


def pack_kernel(first, count, *refs):
    ins, (out, sems) = refs[:-2], refs[-2:]
    peers = out.shape[0]
    each = ins[0].shape[1] // peers
    copy_all(
        [
            (ref.at[:, pl.ds(peer * each + first, count)], out.at[peer, kind])
            for peer in range(peers)
            for kind, ref in enumerate(ins)
        ],
        sems,
    )


def pack(arrays, peers, first, count):
    rows = arrays[0].shape[0]
    kinds = len(arrays)
    anywhere = pl.BlockSpec(memory_space=pl.ANY)
    return pl.pallas_call(
        functools.partial(pack_kernel, first, count),
        in_specs=[anywhere] * kinds,
        out_specs=pl.BlockSpec(memory_space=pltpu.VMEM),
        out_shape=jax.ShapeDtypeStruct((peers, kinds, rows, count), arrays[0].dtype),
        scratch_shapes=[pltpu.SemaphoreType.DMA((peers * kinds,))],
        name="pack",
    )(*arrays)


def unpack_kernel(first, kinds, block, *refs):
    outs, sems = refs[-kinds - 1 : -1], refs[-1]
    peers, _, _, count = block.shape
    each = outs[0].shape[1] // peers
    copy_all(
        [
            (block.at[peer, kind], out.at[:, pl.ds(peer * each + first, count)])
            for peer in range(peers)
            for kind, out in enumerate(outs)
        ],
        sems,
    )


def unpack(block, first, width, held):
    peers, kinds, rows, _ = block.shape
    anywhere = pl.BlockSpec(memory_space=pl.ANY)
    return pl.pallas_call(
        functools.partial(unpack_kernel, first, kinds),
        in_specs=[pl.BlockSpec(memory_space=pltpu.VMEM)] + [anywhere] * len(held),
        out_specs=[anywhere] * kinds,
        out_shape=[jax.ShapeDtypeStruct((rows, width), block.dtype)] * kinds,
        input_output_aliases={1 + kind: kind for kind in range(len(held))},
        scratch_shapes=[pltpu.SemaphoreType.DMA((peers * kinds,))],
        name="unpack",
    )(block, *held)


def attention_kernel(
    widths, meta, seg_key, seg_query, left, own, right, out, window, grads_q, dk, dv, sems
):
    heads, kinds, blocks, rows, _ = window.shape
    peers = own.shape[0]
    edge = left.shape[0]
    scale = HEAD_DIM ** (-0.5)
    factor = scale * float(np.log2(np.e))
    unit, tall = UNIT // rows, TILE // rows
    columns = [slice(head * HEAD_DIM, (head + 1) * HEAD_DIM) for head in range(heads)]
    copies = [
        pltpu.make_async_copy(
            source.at[:, kind, :, columns[head]],
            window.at[head, kind, first : first + source.shape[0]],
            sems.at[head, kind, part],
        )
        for head in range(heads)
        for kind in range(kinds)
        for part, (source, first) in enumerate(
            ((left, 0), (own, edge), (right, edge + peers))
        )
    ]
    for copy in copies:
        copy.start()
    dk[...] = jnp.zeros_like(dk)
    dv[...] = jnp.zeros_like(dv)
    for copy in copies:
        copy.wait()

    def flat(value):
        return value.reshape(value.shape[0] * rows, HEAD_DIM)

    def visit(tile, width):
        lanes = pl.ds(pl.multiple_of(tile * TILE, TILE), TILE)
        first = meta[0, tile]
        marks = seg_key[pl.ds(pl.multiple_of(first * UNIT, UNIT), width * UNIT)]
        inside = jnp.concatenate([marks] * (TILE // 128), axis=1) == seg_query[:, lanes]
        here = pl.ds(tile * tall, tall)
        keys = pl.ds(first * unit, width * unit)
        over = (((1,), (1,)), ((), ()))
        query_terms = []
        for head in range(heads):
            q, g = flat(window[head, 0, here]), flat(window[head, 3, here])
            k, v = flat(window[head, 1, keys]), flat(window[head, 2, keys])
            scores = lax.dot_general(k, q, over, preferred_element_type=jnp.float32)
            dprob = lax.dot_general(v, g, over, preferred_element_type=jnp.float32)
            scores = jnp.where(inside, scores, NEG)
            top = jnp.maximum(jnp.max(scores, axis=0, keepdims=True), FLOOR)
            raised = jnp.exp2((scores - top) * factor)
            total = jnp.sum(raised, axis=0, keepdims=True)
            inverse = jnp.where(total > 0.0, 1.0 / total, 0.0)
            dot = jnp.sum(raised * dprob, axis=0, keepdims=True) * inverse
            probs = raised * inverse
            probs_b = probs.astype(jnp.bfloat16)
            dscore = (probs * (dprob - dot)).astype(jnp.bfloat16)
            shape = (width * unit, rows, HEAD_DIM)
            dv[head, keys] += jnp.dot(probs_b, g, preferred_element_type=jnp.float32).reshape(shape)
            dk[head, keys] += jnp.dot(dscore, q, preferred_element_type=jnp.float32).reshape(shape)
            dq = lax.dot_general(
                dscore, k, (((0,), (0,)), ((), ())), preferred_element_type=jnp.float32
            )
            query_terms.append((dq * scale).astype(jnp.bfloat16).reshape(tall, rows, HEAD_DIM))
        for head in range(heads):
            grads_q[head, here] = query_terms[head]

    def step(tile, carry):
        for width in widths:
            pl.when(meta[1, tile] == width)(functools.partial(visit, tile, width))
        return carry

    lax.fori_loop(0, blocks // tall, step, 0)
    for head in range(heads):
        inner = slice(edge, edge + peers)
        out[:, 0, :, columns[head]] = grads_q[head, inner]
        out[:, 1, :, columns[head]] = (dk[head, inner] * scale).astype(jnp.bfloat16)
        out[:, 2, :, columns[head]] = dv[head, inner].astype(jnp.bfloat16)


def attention(meta, seg_key, seg_query, left, own, right, widths):
    peers, kinds, rows, width = own.shape
    blocks = peers + 2 * left.shape[0]
    heads = width // HEAD_DIM
    elements = heads * blocks * rows * 5 * UNIT
    smem = pl.BlockSpec(memory_space=pltpu.SMEM)
    vmem = pl.BlockSpec(memory_space=pltpu.VMEM)
    anywhere = pl.BlockSpec(memory_space=pl.ANY)
    return pl.pallas_call(
        functools.partial(attention_kernel, widths),
        in_specs=[smem, vmem, vmem, anywhere, anywhere, anywhere],
        out_specs=vmem,
        out_shape=jax.ShapeDtypeStruct((peers, 3, rows, width), jnp.bfloat16),
        scratch_shapes=[
            pltpu.VMEM((heads, kinds, blocks, rows, HEAD_DIM), jnp.bfloat16),
            pltpu.VMEM((heads, blocks, rows, HEAD_DIM), jnp.bfloat16),
            pltpu.VMEM((heads, blocks, rows, HEAD_DIM), jnp.float32),
            pltpu.VMEM((heads, blocks, rows, HEAD_DIM), jnp.float32),
            pltpu.SemaphoreType.DMA((heads, kinds, 3)),
        ],
        cost_estimate=pl.CostEstimate(
            flops=elements * 10 * HEAD_DIM,
            transcendentals=elements,
            bytes_accessed=own.size * 4 + left.size * 4,
        ),
        name="attention",
    )(meta, seg_key, seg_query, left, own, right)


def plan(lengths, me, group, halo, tokens, widths):
    window = group + 2 * halo
    count = lengths.shape[0]
    order = jnp.arange(count, dtype=jnp.int32)
    ends = jnp.sum(jnp.where(order[:, None] <= order[None, :], lengths[:, None], 0), axis=0)
    base = me * group - halo
    at = base + jnp.arange(window, dtype=jnp.int32)
    passed = ends[:, None] <= at[None, :]
    seg = jnp.sum(passed.astype(jnp.int32), axis=0)
    start = jnp.sum(jnp.where(passed, lengths[:, None], 0), axis=0)
    end = jnp.min(jnp.where(passed, tokens, ends[:, None]), axis=0)
    touches = (start < (me + 1) * group) & (end > me * group)
    valid = touches & (at >= 0) & (at < tokens)
    seg_key = jnp.broadcast_to(jnp.where(valid, seg, -1)[:, None], (window, 128))
    seg_query = jnp.where(valid, seg, -2)[None, :]
    first = jnp.min(jnp.where(valid, start - base, window).reshape(-1, TILE), axis=1) // UNIT
    last = jnp.max(jnp.where(valid, end - base, 0).reshape(-1, TILE), axis=1)
    need = (last + UNIT - 1) // UNIT - first
    chosen = jnp.full_like(need, widths[-1])
    for width in reversed(widths):
        chosen = jnp.where(need <= width, width, chosen)
    chosen = jnp.where(last > 0, chosen, 0)
    first = jnp.clip(first, 0, window // UNIT - chosen)
    return jnp.stack([first, chosen]).astype(jnp.int32), seg_key, seg_query


def shards(query, key_in, value_in, out_grad, lengths):
    arrays = (query, key_in, value_in, out_grad)
    plane = ("r", "tp")
    groups = lax.axis_size("g")
    peers = lax.axis_size("r") * lax.axis_size("tp")
    rows, width = query.shape
    each = width // peers
    group = rows * peers
    edge = lax.axis_size("tp")
    halo = rows * edge
    window = group + 2 * halo
    tokens = group * groups
    widths = tuple(w for w in WIDTHS if w < window // UNIT and w <= 10)
    if window // UNIT <= 10:
        widths = widths + (window // UNIT,)
    meta, seg_key, seg_query = plan(lengths, lax.axis_index("g"), group, halo, tokens, widths)
    up = [(i, i + 1) for i in range(groups - 1)]
    down = [(i + 1, i) for i in range(groups - 1)]
    heads = each // HEAD_DIM
    spans = [
        (first * HEAD_DIM, min(CHUNK, heads - first) * HEAD_DIM)
        for first in range(0, heads, CHUNK)
    ]

    def exchange(block, after):
        if after is not None:
            block, _ = lax.optimization_barrier((block, after))
        return lax.all_to_all(block, plane, split_axis=0, concat_axis=0, tiled=True)

    last, gathered = None, []
    for first, count in spans:
        packed = pack(arrays, peers, first, count)
        last = exchange(packed, last)
        gathered.append(last)
    outs = []
    for own, (first, count) in zip(gathered, spans):
        left = lax.ppermute(own[peers - edge :], "g", up)
        right = lax.ppermute(own[:edge], "g", down)
        grads = attention(meta, seg_key, seg_query, left, own, right, widths)
        last = exchange(grads, last)
        outs = unpack(last, first, width, outs)
    return tuple(outs)


def solution(mesh):
    ctx, tp = mesh.devices.shape
    heads_of = lambda width: width // HEAD_DIM

    def run(query, key_in, value_in, out_grad, lengths):
        heads = heads_of(query.shape[1])
        near = max(r for r in range(1, ctx + 1) if ctx % r == 0 and heads % (r * tp) == 0)
        finer = Mesh(mesh.devices.reshape(ctx // near, near, tp), ("g", "r", "tp"))
        placed = P(("g", "r", "tp"), None)
        return jax.shard_map(
            shards,
            mesh=finer,
            in_specs=(placed,) * 4 + (P(),),
            out_specs=(placed,) * 3,
            check_vma=False,
        )(query, key_in, value_in, out_grad, lengths)

    return run
```

time: 212 us -> 199 us (0.939); the launches traced: 212 us -> 196 us
  blocking collectives: 33.2 us -> 0 us
  starting transfers between devices: 42.9 us -> 54.2 us
  waiting for transfers between devices: 70.5 us -> 79.9 us
  other arithmetic: 9.46 us -> 1.67 us
  Pallas kernels: 46.5 us -> 50.4 us
    ppermute x4 -> x0, waiting for transfers between devices: 38.5 us -> none  [the longest x2 23.5 us: shards(): from_right = lax.ppermute(out_left, 'g', down)]
    all_to_all x1 -> x0, blocking collectives: 33.2 us -> none  [shards(): lax.all_to_all(out_own, plane, split_axis=0, concat_axis=0, tiled=True)]
    ppermute x2 -> x3, waiting for transfers between devices: 3.46 us -> 35 us  [shards(): right = lax.ppermute(own[:edge], 'g', down)]
    ppermute x4 -> x0, starting transfers between devices: 22.3 us -> none  [the longest x2 19.7 us: shards(): from_left = lax.ppermute(out_right, 'g', up)]
    all_to_all x3 -> x6, waiting for transfers between devices: 19.4 us -> 41.4 us  [exchange(): return lax.all_to_all(block, plane, split_axis=0, concat_axis=0, tiled=True)]
    ppermute x2 -> x3, starting transfers between devices: 5.45 us -> 25.9 us  [shards(): left = lax.ppermute(own[peers - edge:], 'g', up)]
    all_to_all x3 -> x6, starting transfers between devices: 12.6 us -> 24.4 us  [exchange(): return lax.all_to_all(block, plane, split_axis=0, concat_axis=0, tiled=True)]
    scatter-add x4 -> x0, other arithmetic: 7.78 us -> none  [the longest x2 3.9 us: shards(): out_own = out_own.at[peers - edge:].add(from_right)]
  transfers between devices with their start and end apart: 11 -> 12, of which waited for: 7 -> 9; matrix products, arithmetic and copies ran while one was open for 6% -> 3% of each run, Pallas kernels for 16% -> 23%
where the time goes in v2:
time: 199 us; the launch traced here: 196 us
  waiting for transfers between devices  79.9 us (40%)
  starting transfers between devices  54.2 us (27%)
  Pallas kernels  50.4 us (25%)
  local copies, waits for them, and re-layouts  8.63 us (4%)
    all_to_all x6, waiting for transfers between devices, exchange(): return lax.all_to_all(block, plane, split_axis=0, concat_axis=0, tiled=True)  41.4 us
    ppermute x3, waiting for transfers between devices, shards(): right = lax.ppermute(own[:edge], 'g', down)  35 us
    pallas_call x3, Pallas kernels, attention(): pl.pallas_call(functools.partial(attention_kernel, widths), in_specs=[sme...  33.8 us
    ppermute x3, starting transfers between devices, shards(): left = lax.ppermute(own[peers - edge:], 'g', up)  25.9 us
    all_to_all x6, starting transfers between devices, exchange(): return lax.all_to_all(block, plane, split_axis=0, concat_axis=0, tiled=True)  24.4 us
    pallas_call x3, Pallas kernels, pack(): pl.pallas_call(functools.partial(pack_kernel, first, count), in_specs=[an...  8.85 us
    pallas_call x3, Pallas kernels, unpack(): pl.pallas_call(functools.partial(unpack_kernel, first, kinds), in_specs=[...  7.67 us
    unnamed x20, local copies, waits for them, and re-layouts  3.99 us
  transfers between devices with their start and end apart: 12, of which 9 were waited for; matrix products, arithmetic and copies ran while one was open for 3% of the time, Pallas kernels for 23%

profile of v2, /device:TPU:0, one launch (start us, length us, event | category | flops | bytes accessed | tf_op | source)
XLA Modules:
  0.0 195.9 jit_solution(10577018518378002073)
XLA Ops:
  0.6 3.2 %pack.5 = bf16[8,4,128,256]{3,2,1,0:T(8,128)(2,1)} custom-call(bf16[128,5120]{1,0:T(8,128)(2,1)} %refs_0_.5, bf16[128,5120]{1,0:T(8,128)(2,1)} %refs_1_.5, bf16[128,5120]{1,0:T(8,128)(2,1)} %refs_2_.5, bf16[128,5120]{1,0:T(8,128)(2,1)} %refs_3_.5), custom_call_target="tpu_custom_call" | custom-call | tf_op jit(solution)/shard_map/pack/pallas_call | solution.py:50
  3.8 5.2 %all-to-all-start = ((bf16[8,4,128,256]{3,2,1,0:T(8,128)(2,1)}), bf16[8,4,128,256]{3,2,1,0:T(8,128)(2,1)S(1)}, u32[]{:S(2)}, u32[]{:S(2)}) async-start(bf16[8,4,128,256]{3,2,1,0:T(8,128)(2,1)} %pack.5), calls=%async_computation | async-start | bytes 4194304 | tf_op jit(solution)/shard_map/all_to_all | solution.py:248
  9.0 3.2 %pack.4 = bf16[8,4,128,256]{3,2,1,0:T(8,128)(2,1)} custom-call(bf16[128,5120]{1,0:T(8,128)(2,1)} %refs_0_.5, bf16[128,5120]{1,0:T(8,128)(2,1)} %refs_1_.5, bf16[128,5120]{1,0:T(8,128)(2,1)} %refs_2_.5, bf16[128,5120]{1,0:T(8,128)(2,1)} %refs_3_.5), custom_call_target="tpu_custom_call" | custom-call | tf_op jit(solution)/shard_map/pack/pallas_call | solution.py:50
  12.2 22.5 %all-to-all-done.own = bf16[8,4,128,256]{3,2,1,0:T(8,128)(2,1)S(1)} async-done(((bf16[8,4,128,256]{3,2,1,0:T(8,128)(2,1)}), bf16[8,4,128,256]{3,2,1,0:T(8,128)(2,1)S(1)}, u32[]{:S(2)}, u32[]{:S(2)}) %all-to-all-start) | async-done | bytes 2097184 | tf_op jit(solution)/shard_map/all_to_all | solution.py:248
  34.7 1.3 copy-done.1
  36.1 3.6 %all-to-all-start.1 = ((bf16[8,4,128,256]{3,2,1,0:T(8,128)(2,1)}), bf16[8,4,128,256]{3,2,1,0:T(8,128)(2,1)S(1)}, u32[]{:S(2)}, u32[]{:S(2)}) async-start(bf16[8,4,128,256]{3,2,1,0:T(8,128)(2,1)} %pack.4), calls=%async_computation.1 | async-start | bytes 4194304 | tf_op jit(solution)/shard_map/all_to_all | solution.py:248
  39.7 2.5 %pack.3 = bf16[8,4,128,128]{3,2,1,0:T(8,128)(2,1)} custom-call(bf16[128,5120]{1,0:T(8,128)(2,1)} %refs_0_.5, bf16[128,5120]{1,0:T(8,128)(2,1)} %refs_1_.5, bf16[128,5120]{1,0:T(8,128)(2,1)} %refs_2_.5, bf16[128,5120]{1,0:T(8,128)(2,1)} %refs_3_.5), custom_call_target="tpu_custom_call" | custom-call | tf_op jit(solution)/shard_map/pack/pallas_call | solution.py:50
  42.5 3.1 %fusion.7 = (bf16[4,4,128,256]{3,2,1,0:T(8,128)(2,1)}, bf16[4,4,128,256]{3,2,1,0:T(8,128)(2,1)}) fusion(bf16[8,4,128,256]{3,2,1,0:T(8,128)(2,1)} %copy-done.1), kind=kLoop, calls=%fused_computation.38 | loop fusion | bytes 4194304 | tf_op jit(solution)/shard_map/slice | solution.py:258
  45.5 1.3 collective-permute-start.5
  46.8 5.5 %collective-permute-start.4 = (bf16[4,4,128,256]{3,2,1,0:T(8,128)(2,1)}, bf16[4,4,128,256]{3,2,1,0:T(8,128)(2,1)}, u32[]{:S(2)}, u32[]{:S(2)}) collective-permute-start(bf16[4,4,128,256]{3,2,1,0:T(8,128)(2,1)} %get-tuple-element.33), channel_id=1, source_target_pairs={{0,8},{8,16},{16,24},{1,9},{9,17},{17,25},{2,10},{10,18},{18,26},{... | collective-permute-start | bytes 3145736 | tf_op jit(solution)/shard_map/ppermute | solution.py:257
  52.6 12.7 %all-to-all-done.1.own = bf16[8,4,128,256]{3,2,1,0:T(8,128)(2,1)S(1)} async-done(((bf16[8,4,128,256]{3,2,1,0:T(8,128)(2,1)}), bf16[8,4,128,256]{3,2,1,0:T(8,128)(2,1)S(1)}, u32[]{:S(2)}, u32[]{:S(2)}) %all-to-all-start.1) | async-done | bytes 2097184 | tf_op jit(solution)/shard_map/all_to_all | solution.py:248
  65.3 3.6 %all-to-all-start.2 = ((bf16[8,4,128,128]{3,2,1,0:T(8,128)(2,1)}), bf16[8,4,128,128]{3,2,1,0:T(8,128)(2,1)S(1)}, u32[]{:S(2)}, u32[]{:S(2)}) async-start(bf16[8,4,128,128]{3,2,1,0:T(8,128)(2,1)} %pack.3), calls=%async_computation.2 | async-start | bytes 2097152 | tf_op jit(solution)/shard_map/all_to_all | solution.py:248
  70.1 3.1 %collective-permute-done.5.right = bf16[4,4,128,256]{3,2,1,0:T(8,128)(2,1)} collective-permute-done((bf16[4,4,128,256]{3,2,1,0:T(8,128)(2,1)}, bf16[4,4,128,256]{3,2,1,0:T(8,128)(2,1)}, u32[]{:S(2)}, u32[]{:S(2)}) %collective-permute-start.5) | collective-permute-done | bytes 1048608 | tf_op jit(solution)/shard_map/ppermute | solution.py:258
  73.2 1.2 collective-permute-done.4.left
  74.4 1.3 broadcast_in_dim.74.seg_key
  75.7 12.8 %attention.5 = bf16[8,3,128,256]{3,2,1,0:T(8,128)(2,1)} custom-call(s32[2,8]{1,0:T(2,128)} %pad_add_fusion.meta, s32[2048,128]{1,0:T(8,128)} %broadcast_in_dim.74.seg_key, s32[1,2048]{1,0:T(1,128)} %and_select_fusion.seg_query, bf16[4,4,128,256]{3,2,1,0:T(8,128)(2,1)} %collective-permute-done.4.left, bf16[8,4,128,256]{3,2,1,0:T(8,128)(2,1)} %copy-done.1, ...), custom_call_target="tpu_custom_call" | custom-call | flops 3355443200 | bytes 6291456 | tf_op jit(solution)/shard_map/attention/pallas_call | solution.py:174
  88.5 4.3 %all-to-all-start.3 = ((bf16[8,3,128,256]{3,2,1,0:T(8,128)(2,1)}), bf16[8,3,128,256]{3,2,1,0:T(8,128)(2,1)}, u32[]{:S(2)}, u32[]{:S(2)}) async-start(bf16[8,3,128,256]{3,2,1,0:T(8,128)(2,1)} %attention.5), calls=%async_computation.3 | async-start | bytes 3145728 | tf_op jit(solution)/shard_map/all_to_all | solution.py:248
  93.0 1.3 collective-permute-start.3
  94.3 10.2 %collective-permute-start.2 = (bf16[4,4,128,256]{3,2,1,0:T(8,128)(2,1)S(1)}, bf16[4,4,128,256]{3,2,1,0:T(8,128)(2,1)S(1)}, u32[]{:S(2)}, u32[]{:S(2)}) collective-permute-start(bf16[4,4,128,256]{3,2,1,0:T(8,128)(2,1)S(1)} %get-tuple-element.35), channel_id=1, source_target_pairs={{0,8},{8,16},{16,24},{1,9},{9,17},{17,25},{2,10},{10,18},{18,26},{... | collective-permute-start | bytes 3145736 | tf_op jit(solution)/shard_map/ppermute | solution.py:257
  104.5 21.5 %collective-permute-done.3.right = bf16[4,4,128,256]{3,2,1,0:T(8,128)(2,1)S(1)} collective-permute-done((bf16[4,4,128,256]{3,2,1,0:T(8,128)(2,1)S(1)}, bf16[4,4,128,256]{3,2,1,0:T(8,128)(2,1)S(1)}, u32[]{:S(2)}, u32[]{:S(2)}) %collective-permute-start.3) | collective-permute-done | bytes 1048608 | tf_op jit(solution)/shard_map/ppermute | solution.py:258
  126.0 1.2 collective-permute-done.2.left
  128.2 12.8 %attention.4 = bf16[8,3,128,256]{3,2,1,0:T(8,128)(2,1)} custom-call(s32[2,8]{1,0:T(2,128)} %pad_add_fusion.meta, s32[2048,128]{1,0:T(8,128)} %broadcast_in_dim.74.seg_key, s32[1,2048]{1,0:T(1,128)} %and_select_fusion.seg_query, bf16[4,4,128,256]{3,2,1,0:T(8,128)(2,1)} %copy-done.7, bf16[8,4,128,256]{3,2,1,0:T(8,128)(2,1)} %copy-done, ...), custom_call_target="tpu_custom_call" | custom-call | flops 3355443200 | bytes 6291456 | tf_op jit(solution)/shard_map/attention/pallas_call | solution.py:174
  141.0 3.9 %all-to-all-start.4 = ((bf16[8,3,128,256]{3,2,1,0:T(8,128)(2,1)}), bf16[8,3,128,256]{3,2,1,0:T(8,128)(2,1)S(1)}, u32[]{:S(2)}, u32[]{:S(2)}) async-start(bf16[8,3,128,256]{3,2,1,0:T(8,128)(2,1)} %attention.4), calls=%async_computation.4 | async-start | bytes 3145728 | tf_op jit(solution)/shard_map/all_to_all | solution.py:248
  145.0 1.3 collective-permute-start.1
  146.3 10.2 %collective-permute-start = (bf16[4,4,128,128]{3,2,1,0:T(8,128)(2,1)S(1)}, bf16[4,4,128,128]{3,2,1,0:T(8,128)(2,1)S(1)}, u32[]{:S(2)}, u32[]{:S(2)}) collective-permute-start(bf16[4,4,128,128]{3,2,1,0:T(8,128)(2,1)S(1)} %get-tuple-element.37), channel_id=1, source_target_pairs={{0,8},{8,16},{16,24},{1,9},{9,17},{17,25},{2,10},{10,18},{18,26},{... | collective-permute-start | bytes 1572872 | tf_op jit(solution)/shard_map/ppermute | solution.py:257
  156.5 10.4 %collective-permute-done.1.right = bf16[4,4,128,128]{3,2,1,0:T(8,128)(2,1)S(1)} collective-permute-done((bf16[4,4,128,128]{3,2,1,0:T(8,128)(2,1)S(1)}, bf16[4,4,128,128]{3,2,1,0:T(8,128)(2,1)S(1)}, u32[]{:S(2)}, u32[]{:S(2)}) %collective-permute-start.1) | collective-permute-done | bytes 524320 | tf_op jit(solution)/shard_map/ppermute | solution.py:258
  168.8 8.2 %attention.3 = bf16[8,3,128,128]{3,2,1,0:T(8,128)(2,1)} custom-call(s32[2,8]{1,0:T(2,128)} %pad_add_fusion.meta, s32[2048,128]{1,0:T(8,128)} %broadcast_in_dim.74.seg_key, s32[1,2048]{1,0:T(1,128)} %and_select_fusion.seg_query, bf16[4,4,128,128]{3,2,1,0:T(8,128)(2,1)} %copy-done.9, bf16[8,4,128,128]{3,2,1,0:T(8,128)(2,1)} %copy-done.3, ...), custom_call_target="tpu_custom_call" | custom-call | flops 1677721600 | bytes 3145728 | tf_op jit(solution)/shard_map/attention/pallas_call | solution.py:174
  177.1 3.8 %all-to-all-start.5 = ((bf16[8,3,128,128]{3,2,1,0:T(8,128)(2,1)}), bf16[8,3,128,128]{3,2,1,0:T(8,128)(2,1)S(1)}, u32[]{:S(2)}, u32[]{:S(2)}) async-start(bf16[8,3,128,128]{3,2,1,0:T(8,128)(2,1)} %attention.3), calls=%async_computation.5 | async-start | bytes 1572864 | tf_op jit(solution)/shard_map/all_to_all | solution.py:248
  180.9 2.7 %unpack.3 = (bf16[128,5120]{1,0:T(8,128)(2,1)}, bf16[128,5120]{1,0:T(8,128)(2,1)}, bf16[128,5120]{1,0:T(8,128)(2,1)}) custom-call(bf16[8,3,128,256]{3,2,1,0:T(8,128)(2,1)} %all-to-all-done.3.block), custom_call_target="tpu_custom_call" | custom-call | tf_op jit(solution)/shard_map/unpack/pallas_call | solution.py:77
  183.7 2.7 %unpack.4 = (bf16[128,5120]{1,0:T(8,128)(2,1)}, bf16[128,5120]{1,0:T(8,128)(2,1)}, bf16[128,5120]{1,0:T(8,128)(2,1)}) custom-call(bf16[8,3,128,256]{3,2,1,0:T(8,128)(2,1)} %copy-done.2, bf16[128,5120]{1,0:T(8,128)(2,1)} %get-tuple-element.19.refs_0_, ...), custom_call_target="tpu_custom_call", output_to_operand_aliasing={{0}: (1, {}), {1}: (2, {}), {2}: (3, {})} | custom-call | tf_op jit(solution)/shard_map/unpack/pallas_call | solution.py:77
  186.4 6.2 %all-to-all-done.5.block = bf16[8,3,128,128]{3,2,1,0:T(8,128)(2,1)S(1)} async-done(((bf16[8,3,128,128]{3,2,1,0:T(8,128)(2,1)}), bf16[8,3,128,128]{3,2,1,0:T(8,128)(2,1)S(1)}, u32[]{:S(2)}, u32[]{:S(2)}) %all-to-all-start.5) | async-done | bytes 786464 | tf_op jit(solution)/shard_map/all_to_all | solution.py:248
  193.5 2.2 %unpack.5 = (bf16[128,5120]{1,0:T(8,128)(2,1)}, bf16[128,5120]{1,0:T(8,128)(2,1)}, bf16[128,5120]{1,0:T(8,128)(2,1)}) custom-call(bf16[8,3,128,128]{3,2,1,0:T(8,128)(2,1)} %copy-done.4, bf16[128,5120]{1,0:T(8,128)(2,1)} %get-tuple-element.22.refs_0_, ...), custom_call_target="tpu_custom_call", output_to_operand_aliasing={{0}: (1, {}), {1}: (2, {}), {2}: (3, {})} | custom-call | tf_op jit(solution)/shard_map/unpack/pallas_call | solution.py:77
  (36 shorter events, 5.8 us)
Async XLA Ops:
  3.8 30.9 %all-to-all-start = ((bf16[8,4,128,256]{3,2,1,0:T(8,128)(2,1)}), bf16[8,4,128,256]{3,2,1,0:T(8,128)(2,1)S(1)}, u32[]{:S(2)}, u32[]{:S(2)}) async-start(bf16[8,4,128,256]{3,2,1,0:T(8,128)(2,1)} %pack.5), calls=%async_computation | async-start | bytes 4194304 | tf_op jit(solution)/shard_map/all_to_all | solution.py:248
  34.7 1.3 copy-start.1
  36.1 29.2 %all-to-all-start.1 = ((bf16[8,4,128,256]{3,2,1,0:T(8,128)(2,1)}), bf16[8,4,128,256]{3,2,1,0:T(8,128)(2,1)S(1)}, u32[]{:S(2)}, u32[]{:S(2)}) async-start(bf16[8,4,128,256]{3,2,1,0:T(8,128)(2,1)} %pack.4), calls=%async_computation.1 | async-start | bytes 4194304 | tf_op jit(solution)/shard_map/all_to_all | solution.py:248
  39.7 2.5 %copy-start.5 = (s32[32]{0:T(128)S(1)}, s32[32]{0:T(128)}, u32[]{:S(2)}) copy-start(s32[32]{0:T(128)} %param.9) | copy-start | bytes 388
  45.5 27.6 %collective-permute-start.5 = (bf16[4,4,128,256]{3,2,1,0:T(8,128)(2,1)}, bf16[4,4,128,256]{3,2,1,0:T(8,128)(2,1)}, u32[]{:S(2)}, u32[]{:S(2)}) collective-permute-start(bf16[4,4,128,256]{3,2,1,0:T(8,128)(2,1)} %get-tuple-element.32), channel_id=1, source_target_pairs={{8,0},{16,8},{24,16},{9,1},{17,9},{25,17},{10,2},{18,10},{26,18},{... | collective-permute-start | bytes 3145736 | tf_op jit(solution)/shard_map/ppermute | solution.py:258
  46.8 27.5 %collective-permute-start.4 = (bf16[4,4,128,256]{3,2,1,0:T(8,128)(2,1)}, bf16[4,4,128,256]{3,2,1,0:T(8,128)(2,1)}, u32[]{:S(2)}, u32[]{:S(2)}) collective-permute-start(bf16[4,4,128,256]{3,2,1,0:T(8,128)(2,1)} %get-tuple-element.33), channel_id=1, source_target_pairs={{0,8},{8,16},{16,24},{1,9},{9,17},{17,25},{2,10},{10,18},{18,26},{... | collective-permute-start | bytes 3145736 | tf_op jit(solution)/shard_map/ppermute | solution.py:257
  65.3 27.5 %copy-start = (bf16[8,4,128,256]{3,2,1,0:T(8,128)(2,1)}, bf16[8,4,128,256]{3,2,1,0:T(8,128)(2,1)S(1)}, u32[]{:S(2)}) copy-start(bf16[8,4,128,256]{3,2,1,0:T(8,128)(2,1)S(1)} %all-to-all-done.1.own) | copy-start | bytes 6291460
  65.3 23.2 %all-to-all-start.2 = ((bf16[8,4,128,128]{3,2,1,0:T(8,128)(2,1)}), bf16[8,4,128,128]{3,2,1,0:T(8,128)(2,1)S(1)}, u32[]{:S(2)}, u32[]{:S(2)}) async-start(bf16[8,4,128,128]{3,2,1,0:T(8,128)(2,1)} %pack.3), calls=%async_computation.2 | async-start | bytes 2097152 | tf_op jit(solution)/shard_map/all_to_all | solution.py:248
  88.5 56.3 %copy-start.3 = (bf16[8,4,128,128]{3,2,1,0:T(8,128)(2,1)}, bf16[8,4,128,128]{3,2,1,0:T(8,128)(2,1)S(1)}, u32[]{:S(2)}) copy-start(bf16[8,4,128,128]{3,2,1,0:T(8,128)(2,1)S(1)} %all-to-all-done.2.own) | copy-start | bytes 3145732
  88.5 52.5 %all-to-all-start.3 = ((bf16[8,3,128,256]{3,2,1,0:T(8,128)(2,1)}), bf16[8,3,128,256]{3,2,1,0:T(8,128)(2,1)}, u32[]{:S(2)}, u32[]{:S(2)}) async-start(bf16[8,3,128,256]{3,2,1,0:T(8,128)(2,1)} %attention.5), calls=%async_computation.3 | async-start | bytes 3145728 | tf_op jit(solution)/shard_map/all_to_all | solution.py:248
  93.0 33.0 %collective-permute-start.3 = (bf16[4,4,128,256]{3,2,1,0:T(8,128)(2,1)S(1)}, bf16[4,4,128,256]{3,2,1,0:T(8,128)(2,1)S(1)}, u32[]{:S(2)}, u32[]{:S(2)}) collective-permute-start(bf16[4,4,128,256]{3,2,1,0:T(8,128)(2,1)S(1)} %get-tuple-element.34), channel_id=1, source_target_pairs={{8,0},{16,8},{24,16},{9,1},{17,9},{25,17},{10,2},{18,10},{26,18},{... | collective-permute-start | bytes 3145736 | tf_op jit(solution)/shard_map/ppermute | solution.py:258
  94.3 32.9 %collective-permute-start.2 = (bf16[4,4,128,256]{3,2,1,0:T(8,128)(2,1)S(1)}, bf16[4,4,128,256]{3,2,1,0:T(8,128)(2,1)S(1)}, u32[]{:S(2)}, u32[]{:S(2)}) collective-permute-start(bf16[4,4,128,256]{3,2,1,0:T(8,128)(2,1)S(1)} %get-tuple-element.35), channel_id=1, source_target_pairs={{0,8},{8,16},{16,24},{1,9},{9,17},{17,25},{2,10},{10,18},{18,26},{... | collective-permute-start | bytes 3145736 | tf_op jit(solution)/shard_map/ppermute | solution.py:257
  126.0 1.2 copy-start.6
  127.2 1.0 copy-start.7
  141.0 36.1 %all-to-all-start.4 = ((bf16[8,3,128,256]{3,2,1,0:T(8,128)(2,1)}), bf16[8,3,128,256]{3,2,1,0:T(8,128)(2,1)S(1)}, u32[]{:S(2)}, u32[]{:S(2)}) async-start(bf16[8,3,128,256]{3,2,1,0:T(8,128)(2,1)} %attention.4), calls=%async_computation.4 | async-start | bytes 3145728 | tf_op jit(solution)/shard_map/all_to_all | solution.py:248
  145.0 21.9 %collective-permute-start.1 = (bf16[4,4,128,128]{3,2,1,0:T(8,128)(2,1)S(1)}, bf16[4,4,128,128]{3,2,1,0:T(8,128)(2,1)S(1)}, u32[]{:S(2)}, u32[]{:S(2)}) collective-permute-start(bf16[4,4,128,128]{3,2,1,0:T(8,128)(2,1)S(1)} %get-tuple-element.36), channel_id=1, source_target_pairs={{8,0},{16,8},{24,16},{9,1},{17,9},{25,17},{10,2},{18,10},{26,18},{... | collective-permute-start | bytes 1572872 | tf_op jit(solution)/shard_map/ppermute | solution.py:258
  146.3 21.8 %collective-permute-start = (bf16[4,4,128,128]{3,2,1,0:T(8,128)(2,1)S(1)}, bf16[4,4,128,128]{3,2,1,0:T(8,128)(2,1)S(1)}, u32[]{:S(2)}, u32[]{:S(2)}) collective-permute-start(bf16[4,4,128,128]{3,2,1,0:T(8,128)(2,1)S(1)} %get-tuple-element.37), channel_id=1, source_target_pairs={{0,8},{8,16},{16,24},{1,9},{9,17},{17,25},{2,10},{10,18},{18,26},{... | collective-permute-start | bytes 1572872 | tf_op jit(solution)/shard_map/ppermute | solution.py:257
  166.9 1.2 copy-start.8
  168.0 0.8 copy-start.9
  177.1 6.6 %copy-start.2 = (bf16[8,3,128,256]{3,2,1,0:T(8,128)(2,1)}, bf16[8,3,128,256]{3,2,1,0:T(8,128)(2,1)S(1)}, u32[]{:S(2)}) copy-start(bf16[8,3,128,256]{3,2,1,0:T(8,128)(2,1)S(1)} %all-to-all-done.4.block) | copy-start | bytes 4718596
  177.1 15.5 %all-to-all-start.5 = ((bf16[8,3,128,128]{3,2,1,0:T(8,128)(2,1)}), bf16[8,3,128,128]{3,2,1,0:T(8,128)(2,1)S(1)}, u32[]{:S(2)}, u32[]{:S(2)}) async-start(bf16[8,3,128,128]{3,2,1,0:T(8,128)(2,1)} %attention.3), calls=%async_computation.5 | async-start | bytes 1572864 | tf_op jit(solution)/shard_map/all_to_all | solution.py:248
  192.6 0.9 copy-start.4

commit v3 on v2

--- a/solution.py
+++ b/solution.py
@@ -15,6 +15,7 @@
 UNIT = 128
 CHUNK = 2
 TILE = 256
+STRIDE = 2
 WIDTHS = (4, 5, 6, 8, 10)
 
 
@@ -46,7 +47,7 @@
 def pack(arrays, peers, first, count):
     rows = arrays[0].shape[0]
     kinds = len(arrays)
-    anywhere = pl.BlockSpec(memory_space=pl.ANY)
+    anywhere = pl.BlockSpec(memory_space=pltpu.HBM)
     return pl.pallas_call(
         functools.partial(pack_kernel, first, count),
         in_specs=[anywhere] * kinds,
@@ -73,7 +74,7 @@
 
 def unpack(block, first, width, held):
     peers, kinds, rows, _ = block.shape
-    anywhere = pl.BlockSpec(memory_space=pl.ANY)
+    anywhere = pl.BlockSpec(memory_space=pltpu.HBM)
     return pl.pallas_call(
         functools.partial(unpack_kernel, first, kinds),
         in_specs=[pl.BlockSpec(memory_space=pltpu.VMEM)] + [anywhere] * len(held),
@@ -81,12 +82,28 @@
         out_shape=[jax.ShapeDtypeStruct((rows, width), block.dtype)] * kinds,
         input_output_aliases={1 + kind: kind for kind in range(len(held))},
         scratch_shapes=[pltpu.SemaphoreType.DMA((peers * kinds,))],
+        compiler_params=pltpu.CompilerParams(vmem_limit_bytes=8 << 20),
         name="unpack",
     )(block, *held)
 
 
 def attention_kernel(
-    widths, meta, seg_key, seg_query, left, own, right, out, window, grads_q, dk, dv, sems
+    widths,
+    meta,
+    marks_in,
+    seg_query,
+    left,
+    own,
+    right,
+    result,
+    seg_key,
+    out,
+    window,
+    grads_q,
+    dk,
+    dv,
+    sems,
+    edge_sems,
 ):
     heads, kinds, blocks, rows, _ = window.shape
     peers = own.shape[0]
@@ -107,6 +124,7 @@
             ((left, 0), (own, edge), (right, edge + peers))
         )
     ]
+    copies.append(pltpu.make_async_copy(marks_in, seg_key, edge_sems.at[0]))
     for copy in copies:
         copy.start()
     dk[...] = jnp.zeros_like(dk)
@@ -123,29 +141,56 @@
         marks = seg_key[pl.ds(pl.multiple_of(first * UNIT, UNIT), width * UNIT)]
         inside = jnp.concatenate([marks] * (TILE // 128), axis=1) == seg_query[:, lanes]
         here = pl.ds(tile * tall, tall)
-        keys = pl.ds(first * unit, width * unit)
         over = (((1,), (1,)), ((), ()))
-        query_terms = []
+        down = (((0,), (0,)), ((), ()))
+        pieces = [
+            (at, min(STRIDE, width - at)) for at in range(0, width, STRIDE)
+        ]
+
+        def span(at, count):
+            return pl.ds((first + at) * unit, count * unit)
+
+        def dot(left, right, dims):
+            return lax.dot_general(left, right, dims, preferred_element_type=jnp.float32)
+
+        plain = (((1,), (0,)), ((), ()))
+        query_terms, held = [], []
+        for head in range(heads):
+            q = flat(window[head, 0, here])
+            scores, top = [], FLOOR
+            for at, count in pieces:
+                piece = dot(flat(window[head, 1, span(at, count)]), q, over)
+                piece = jnp.where(inside[at * UNIT : (at + count) * UNIT], piece, NEG)
+                scores.append(piece)
+                top = jnp.maximum(top, jnp.max(piece, axis=0, keepdims=True))
+            held.append((scores, top))
+        middle = []
+        for head in range(heads):
+            g = flat(window[head, 3, here])
+            scores, top = held[head]
+            raised, dprobs, total, product = [], [], 0.0, 0.0
+            for (at, count), piece in zip(pieces, scores):
+                dprob = dot(flat(window[head, 2, span(at, count)]), g, over)
+                piece = jnp.exp2((piece - top) * factor)
+                total = total + jnp.sum(piece, axis=0, keepdims=True)
+                product = product + jnp.sum(piece * dprob, axis=0, keepdims=True)
+                raised.append(piece)
+                dprobs.append(dprob)
+            middle.append((raised, dprobs, total, product))
         for head in range(heads):
             q, g = flat(window[head, 0, here]), flat(window[head, 3, here])
-            k, v = flat(window[head, 1, keys]), flat(window[head, 2, keys])
-            scores = lax.dot_general(k, q, over, preferred_element_type=jnp.float32)
-            dprob = lax.dot_general(v, g, over, preferred_element_type=jnp.float32)
-            scores = jnp.where(inside, scores, NEG)
-            top = jnp.maximum(jnp.max(scores, axis=0, keepdims=True), FLOOR)
-            raised = jnp.exp2((scores - top) * factor)
-            total = jnp.sum(raised, axis=0, keepdims=True)
+            raised, dprobs, total, product = middle[head]
             inverse = jnp.where(total > 0.0, 1.0 / total, 0.0)
-            dot = jnp.sum(raised * dprob, axis=0, keepdims=True) * inverse
-            probs = raised * inverse
-            probs_b = probs.astype(jnp.bfloat16)
-            dscore = (probs * (dprob - dot)).astype(jnp.bfloat16)
-            shape = (width * unit, rows, HEAD_DIM)
-            dv[head, keys] += jnp.dot(probs_b, g, preferred_element_type=jnp.float32).reshape(shape)
-            dk[head, keys] += jnp.dot(dscore, q, preferred_element_type=jnp.float32).reshape(shape)
-            dq = lax.dot_general(
-                dscore, k, (((0,), (0,)), ((), ())), preferred_element_type=jnp.float32
-            )
+            product = product * inverse
+            dq = 0.0
+            for (at, count), piece, dprob in zip(pieces, raised, dprobs):
+                probs = piece * inverse
+                dscore = (probs * (dprob - product)).astype(jnp.bfloat16)
+                keys = span(at, count)
+                shape = (count * unit, rows, HEAD_DIM)
+                dv[head, keys] += dot(probs.astype(jnp.bfloat16), g, plain).reshape(shape)
+                dk[head, keys] += dot(dscore, q, plain).reshape(shape)
+                dq = dq + dot(dscore, flat(window[head, 1, keys]), down)
             query_terms.append((dq * scale).astype(jnp.bfloat16).reshape(tall, rows, HEAD_DIM))
         for head in range(heads):
             grads_q[head, here] = query_terms[head]
@@ -161,6 +206,9 @@
         out[:, 0, :, columns[head]] = grads_q[head, inner]
         out[:, 1, :, columns[head]] = (dk[head, inner] * scale).astype(jnp.bfloat16)
         out[:, 2, :, columns[head]] = dv[head, inner].astype(jnp.bfloat16)
+    leaving = pltpu.make_async_copy(out, result, edge_sems.at[1])
+    leaving.start()
+    leaving.wait()
 
 
 def attention(meta, seg_key, seg_query, left, own, right, widths):
@@ -170,26 +218,38 @@
     elements = heads * blocks * rows * 5 * UNIT
     smem = pl.BlockSpec(memory_space=pltpu.SMEM)
     vmem = pl.BlockSpec(memory_space=pltpu.VMEM)
+    outer = pl.BlockSpec(memory_space=pltpu.HBM)
     anywhere = pl.BlockSpec(memory_space=pl.ANY)
     return pl.pallas_call(
         functools.partial(attention_kernel, widths),
-        in_specs=[smem, vmem, vmem, anywhere, anywhere, anywhere],
-        out_specs=vmem,
-        out_shape=jax.ShapeDtypeStruct((peers, 3, rows, width), jnp.bfloat16),
+        in_specs=[smem, outer, vmem, anywhere, anywhere, anywhere],
+        out_specs=outer,
+        out_shape=pltpu.HBM((peers, 3, rows, width), jnp.bfloat16),
         scratch_shapes=[
+            pltpu.VMEM(seg_key.shape, jnp.int32),
+            pltpu.VMEM((peers, 3, rows, width), jnp.bfloat16),
             pltpu.VMEM((heads, kinds, blocks, rows, HEAD_DIM), jnp.bfloat16),
             pltpu.VMEM((heads, blocks, rows, HEAD_DIM), jnp.bfloat16),
             pltpu.VMEM((heads, blocks, rows, HEAD_DIM), jnp.float32),
             pltpu.VMEM((heads, blocks, rows, HEAD_DIM), jnp.float32),
             pltpu.SemaphoreType.DMA((heads, kinds, 3)),
+            pltpu.SemaphoreType.DMA((2,)),
         ],
         cost_estimate=pl.CostEstimate(
             flops=elements * 10 * HEAD_DIM,
             transcendentals=elements,
             bytes_accessed=own.size * 4 + left.size * 4,
         ),
+        compiler_params=pltpu.CompilerParams(vmem_limit_bytes=32 << 20),
         name="attention",
-    )(meta, seg_key, seg_query, left, own, right)
+    )(
+        meta,
+        pltpu.with_memory_space_constraint(seg_key, pltpu.HBM),
+        seg_query,
+        left,
+        own,
+        right,
+    )
 
 
 def plan(lengths, me, group, halo, tokens, widths):
@@ -237,9 +297,9 @@
     up = [(i, i + 1) for i in range(groups - 1)]
     down = [(i + 1, i) for i in range(groups - 1)]
     heads = each // HEAD_DIM
+    cuts = [0] + list(range(heads % CHUNK or CHUNK, heads + 1, CHUNK))
     spans = [
-        (first * HEAD_DIM, min(CHUNK, heads - first) * HEAD_DIM)
-        for first in range(0, heads, CHUNK)
+        (first * HEAD_DIM, (last - first) * HEAD_DIM) for first, last in zip(cuts, cuts[1:])
     ]
 
     def exchange(block, after):

time: 199 us -> 188 us (0.945)
  the two profiles are of different devices: /device:TPU:0 before, /device:TPU:8 now
where the time goes in v3:
time: 188 us; the launch traced here: 187 us
  waiting for transfers between devices  85.6 us (46%)
  Pallas kernels  52.3 us (28%)
  starting transfers between devices  41.2 us (22%)
  local copies, waits for them, and re-layouts  6.62 us (4%)
    all_to_all x6, waiting for transfers between devices, exchange(): return lax.all_to_all(block, plane, split_axis=0, concat_axis=0, tiled=True)  49.9 us
    pallas_call x3, Pallas kernels, attention(): pl.pallas_call(functools.partial(attention_kernel, widths), in_specs=[sme...  39.7 us
    ppermute x3, waiting for transfers between devices, shards(): right = lax.ppermute(own[:edge], 'g', down)  29.3 us
    all_to_all x6, starting transfers between devices, exchange(): return lax.all_to_all(block, plane, split_axis=0, concat_axis=0, tiled=True)  23.5 us
    ppermute x3, starting transfers between devices, shards(): left = lax.ppermute(own[peers - edge:], 'g', up)  11.1 us
    pallas_call x3, Pallas kernels, pack(): pl.pallas_call(functools.partial(pack_kernel, first, count), in_specs=[an...  8.82 us
    ppermute x3, starting transfers between devices, shards(): right = lax.ppermute(own[:edge], 'g', down)  6.65 us
    ppermute x3, waiting for transfers between devices, shards(): left = lax.ppermute(own[peers - edge:], 'g', up)  6.38 us
  transfers between devices with their start and end apart: 12, of which 9 were waited for; matrix products, arithmetic and copies ran while one was open for 3% of the time, Pallas kernels for 26%

profile of v3, /device:TPU:8, one launch (start us, length us, event | category | flops | bytes accessed | tf_op | source)
XLA Modules:
  0.0 187.3 jit_solution(1013441372743417033)
XLA Ops:
  0.6 2.4 %pack.5 = bf16[8,4,128,128]{3,2,1,0:T(8,128)(2,1)} custom-call(bf16[128,5120]{1,0:T(8,128)(2,1)} %refs_0_.5, bf16[128,5120]{1,0:T(8,128)(2,1)} %refs_1_.5, bf16[128,5120]{1,0:T(8,128)(2,1)} %refs_2_.5, bf16[128,5120]{1,0:T(8,128)(2,1)} %refs_3_.5), custom_call_target="tpu_custom_call" | custom-call | tf_op jit(solution)/shard_map/pack/pallas_call | solution.py:51
  3.1 3.7 %all-to-all-start = ((bf16[8,4,128,128]{3,2,1,0:T(8,128)(2,1)}), bf16[8,4,128,128]{3,2,1,0:T(8,128)(2,1)S(1)}, u32[]{:S(2)}, u32[]{:S(2)}) async-start(bf16[8,4,128,128]{3,2,1,0:T(8,128)(2,1)} %pack.5), calls=%async_computation | async-start | bytes 2097152 | tf_op jit(solution)/shard_map/all_to_all | solution.py:308
  6.8 3.2 %pack.4 = bf16[8,4,128,256]{3,2,1,0:T(8,128)(2,1)} custom-call(bf16[128,5120]{1,0:T(8,128)(2,1)} %refs_0_.5, bf16[128,5120]{1,0:T(8,128)(2,1)} %refs_1_.5, bf16[128,5120]{1,0:T(8,128)(2,1)} %refs_2_.5, bf16[128,5120]{1,0:T(8,128)(2,1)} %refs_3_.5), custom_call_target="tpu_custom_call" | custom-call | tf_op jit(solution)/shard_map/pack/pallas_call | solution.py:51
  10.0 11.3 %all-to-all-done.own = bf16[8,4,128,128]{3,2,1,0:T(8,128)(2,1)S(1)} async-done(((bf16[8,4,128,128]{3,2,1,0:T(8,128)(2,1)}), bf16[8,4,128,128]{3,2,1,0:T(8,128)(2,1)S(1)}, u32[]{:S(2)}, u32[]{:S(2)}) %all-to-all-start) | async-done | bytes 1048608 | tf_op jit(solution)/shard_map/all_to_all | solution.py:308
  21.3 3.6 %all-to-all-start.1 = ((bf16[8,4,128,256]{3,2,1,0:T(8,128)(2,1)}), bf16[8,4,128,256]{3,2,1,0:T(8,128)(2,1)S(1)}, u32[]{:S(2)}, u32[]{:S(2)}) async-start(bf16[8,4,128,256]{3,2,1,0:T(8,128)(2,1)} %pack.4), calls=%async_computation.1 | async-start | bytes 4194304 | tf_op jit(solution)/shard_map/all_to_all | solution.py:308
  24.9 3.2 %pack.3 = bf16[8,4,128,256]{3,2,1,0:T(8,128)(2,1)} custom-call(bf16[128,5120]{1,0:T(8,128)(2,1)} %refs_0_.5, bf16[128,5120]{1,0:T(8,128)(2,1)} %refs_1_.5, bf16[128,5120]{1,0:T(8,128)(2,1)} %refs_2_.5, bf16[128,5120]{1,0:T(8,128)(2,1)} %refs_3_.5), custom_call_target="tpu_custom_call" | custom-call | tf_op jit(solution)/shard_map/pack/pallas_call | solution.py:51
  28.4 22.1 %all-to-all-done.1.own = bf16[8,4,128,256]{3,2,1,0:T(8,128)(2,1)S(1)} async-done(((bf16[8,4,128,256]{3,2,1,0:T(8,128)(2,1)}), bf16[8,4,128,256]{3,2,1,0:T(8,128)(2,1)S(1)}, u32[]{:S(2)}, u32[]{:S(2)}) %all-to-all-start.1) | async-done | bytes 2097184 | tf_op jit(solution)/shard_map/all_to_all | solution.py:308
  50.5 4.4 %all-to-all-start.2 = ((bf16[8,4,128,256]{3,2,1,0:T(8,128)(2,1)}), bf16[8,4,128,256]{3,2,1,0:T(8,128)(2,1)}, u32[]{:S(2)}, u32[]{:S(2)}) async-start(bf16[8,4,128,256]{3,2,1,0:T(8,128)(2,1)} %pack.3), calls=%async_computation.2 | async-start | bytes 4194304 | tf_op jit(solution)/shard_map/all_to_all | solution.py:308
  55.2 2.4 %collective-permute-start.5 = (bf16[4,4,128,128]{3,2,1,0:T(8,128)(2,1)S(1)}, bf16[4,4,128,128]{3,2,1,0:T(8,128)(2,1)S(1)}, u32[]{:S(2)}, u32[]{:S(2)}) collective-permute-start(bf16[4,4,128,128]{3,2,1,0:T(8,128)(2,1)S(1)} %get-tuple-element.36), channel_id=1, source_target_pairs={{8,0},{16,8},{24,16},{9,1},{17,9},{25,17},{10,2},{18,10},{26,18},{... | collective-permute-start | bytes 1572872 | tf_op jit(solution)/shard_map/ppermute | solution.py:318
  57.6 3.5 %collective-permute-start.4 = (bf16[4,4,128,128]{3,2,1,0:T(8,128)(2,1)S(1)}, bf16[4,4,128,128]{3,2,1,0:T(8,128)(2,1)S(1)}, u32[]{:S(2)}, u32[]{:S(2)}) collective-permute-start(bf16[4,4,128,128]{3,2,1,0:T(8,128)(2,1)S(1)} %get-tuple-element.37), channel_id=1, source_target_pairs={{0,8},{8,16},{16,24},{1,9},{9,17},{17,25},{2,10},{10,18},{18,26},{... | collective-permute-start | bytes 1572872 | tf_op jit(solution)/shard_map/ppermute | solution.py:317
  61.1 1.5 fusion.7
  62.6 2.4 %collective-permute-start.3 = (bf16[4,4,128,256]{3,2,1,0:T(8,128)(2,1)}, bf16[4,4,128,256]{3,2,1,0:T(8,128)(2,1)}, u32[]{:S(2)}, u32[]{:S(2)}) collective-permute-start(bf16[4,4,128,256]{3,2,1,0:T(8,128)(2,1)} %get-tuple-element.32), channel_id=1, source_target_pairs={{8,0},{16,8},{24,16},{9,1},{17,9},{25,17},{10,2},{18,10},{26,18},{... | collective-permute-start | bytes 3145736 | tf_op jit(solution)/shard_map/ppermute | solution.py:318
  65.0 3.5 %collective-permute-start.2 = (bf16[4,4,128,256]{3,2,1,0:T(8,128)(2,1)}, bf16[4,4,128,256]{3,2,1,0:T(8,128)(2,1)}, u32[]{:S(2)}, u32[]{:S(2)}) collective-permute-start(bf16[4,4,128,256]{3,2,1,0:T(8,128)(2,1)} %get-tuple-element.33), channel_id=1, source_target_pairs={{0,8},{8,16},{16,24},{1,9},{9,17},{17,25},{2,10},{10,18},{18,26},{... | collective-permute-start | bytes 3145736 | tf_op jit(solution)/shard_map/ppermute | solution.py:317
  68.5 3.4 %collective-permute-done.5.right = bf16[4,4,128,128]{3,2,1,0:T(8,128)(2,1)S(1)} collective-permute-done((bf16[4,4,128,128]{3,2,1,0:T(8,128)(2,1)S(1)}, bf16[4,4,128,128]{3,2,1,0:T(8,128)(2,1)S(1)}, u32[]{:S(2)}, u32[]{:S(2)}) %collective-permute-start.5) | collective-permute-done | bytes 524320 | tf_op jit(solution)/shard_map/ppermute | solution.py:318
  71.9 2.4 %collective-permute-done.4.left = bf16[4,4,128,128]{3,2,1,0:T(8,128)(2,1)S(1)} collective-permute-done((bf16[4,4,128,128]{3,2,1,0:T(8,128)(2,1)S(1)}, bf16[4,4,128,128]{3,2,1,0:T(8,128)(2,1)S(1)}, u32[]{:S(2)}, u32[]{:S(2)}) %collective-permute-start.4) | collective-permute-done | bytes 524320 | tf_op jit(solution)/shard_map/ppermute | solution.py:317
  74.3 1.3 broadcast_in_dim.74.marks_in
  75.6 9.6 %attention.5 = bf16[8,3,128,128]{3,2,1,0:T(8,128)(2,1)} custom-call(s32[2,8]{1,0:T(2,128)S(1)} %pad_add_fusion.meta, s32[2048,128]{1,0:T(8,128)} %broadcast_in_dim.74.marks_in, s32[1,2048]{1,0:T(1,128)S(1)} %and_select_fusion.seg_query, bf16[4,4,128,128]{3,2,1,0:T(8,128)(2,1)S(1)} %collective-permute-done.4.left, ...), custom_call_target="tpu_custom_call" | custom-call | flops 1677721600 | bytes 3145728 | tf_op jit(solution)/shard_map/attention/pallas_call | solution.py:223
  85.2 4.1 %all-to-all-start.3 = ((bf16[8,3,128,128]{3,2,1,0:T(8,128)(2,1)}), bf16[8,3,128,128]{3,2,1,0:T(8,128)(2,1)S(1)}, u32[]{:S(2)}, u32[]{:S(2)}) async-start(bf16[8,3,128,128]{3,2,1,0:T(8,128)(2,1)} %attention.5), calls=%async_computation.3 | async-start | bytes 1572864 | tf_op jit(solution)/shard_map/all_to_all | solution.py:308
  89.3 4.5 %collective-permute-done.3.right = bf16[4,4,128,256]{3,2,1,0:T(8,128)(2,1)} collective-permute-done((bf16[4,4,128,256]{3,2,1,0:T(8,128)(2,1)}, bf16[4,4,128,256]{3,2,1,0:T(8,128)(2,1)}, u32[]{:S(2)}, u32[]{:S(2)}) %collective-permute-start.3) | collective-permute-done | bytes 1048608 | tf_op jit(solution)/shard_map/ppermute | solution.py:318
  93.9 2.1 %collective-permute-done.2.left = bf16[4,4,128,256]{3,2,1,0:T(8,128)(2,1)} collective-permute-done((bf16[4,4,128,256]{3,2,1,0:T(8,128)(2,1)}, bf16[4,4,128,256]{3,2,1,0:T(8,128)(2,1)}, u32[]{:S(2)}, u32[]{:S(2)}) %collective-permute-start.2) | collective-permute-done | bytes 1048608 | tf_op jit(solution)/shard_map/ppermute | solution.py:317
  96.0 15.1 %attention.4 = bf16[8,3,128,256]{3,2,1,0:T(8,128)(2,1)} custom-call(s32[2,8]{1,0:T(2,128)S(1)} %pad_add_fusion.meta, s32[2048,128]{1,0:T(8,128)} %broadcast_in_dim.74.marks_in, s32[1,2048]{1,0:T(1,128)S(1)} %and_select_fusion.seg_query, bf16[4,4,128,256]{3,2,1,0:T(8,128)(2,1)} %collective-permute-done.2.left, ...), custom_call_target="tpu_custom_call" | custom-call | flops 3355443200 | bytes 6291456 | tf_op jit(solution)/shard_map/attention/pallas_call | solution.py:223
  112.0 3.8 %all-to-all-start.4 = ((bf16[8,3,128,256]{3,2,1,0:T(8,128)(2,1)}), bf16[8,3,128,256]{3,2,1,0:T(8,128)(2,1)S(1)}, u32[]{:S(2)}, u32[]{:S(2)}) async-start(bf16[8,3,128,256]{3,2,1,0:T(8,128)(2,1)} %attention.4), calls=%async_computation.4 | async-start | bytes 3145728 | tf_op jit(solution)/shard_map/all_to_all | solution.py:308
  115.8 1.7 fusion.8
  117.5 1.9 %collective-permute-start.1 = (bf16[4,4,128,256]{3,2,1,0:T(8,128)(2,1)S(1)}, bf16[4,4,128,256]{3,2,1,0:T(8,128)(2,1)S(1)}, u32[]{:S(2)}, u32[]{:S(2)}) collective-permute-start(bf16[4,4,128,256]{3,2,1,0:T(8,128)(2,1)S(1)} %get-tuple-element.34), channel_id=1, source_target_pairs={{8,0},{16,8},{24,16},{9,1},{17,9},{25,17},{10,2},{18,10},{26,18},{... | collective-permute-start | bytes 3145736 | tf_op jit(solution)/shard_map/ppermute | solution.py:318
  119.4 4.1 %collective-permute-start = (bf16[4,4,128,256]{3,2,1,0:T(8,128)(2,1)S(1)}, bf16[4,4,128,256]{3,2,1,0:T(8,128)(2,1)S(1)}, u32[]{:S(2)}, u32[]{:S(2)}) collective-permute-start(bf16[4,4,128,256]{3,2,1,0:T(8,128)(2,1)S(1)} %get-tuple-element.35), channel_id=1, source_target_pairs={{0,8},{8,16},{16,24},{1,9},{9,17},{17,25},{2,10},{10,18},{18,26},{... | collective-permute-start | bytes 3145736 | tf_op jit(solution)/shard_map/ppermute | solution.py:317
  123.6 21.4 %collective-permute-done.1.right = bf16[4,4,128,256]{3,2,1,0:T(8,128)(2,1)S(1)} collective-permute-done((bf16[4,4,128,256]{3,2,1,0:T(8,128)(2,1)S(1)}, bf16[4,4,128,256]{3,2,1,0:T(8,128)(2,1)S(1)}, u32[]{:S(2)}, u32[]{:S(2)}) %collective-permute-start.1) | collective-permute-done | bytes 1048608 | tf_op jit(solution)/shard_map/ppermute | solution.py:318
  145.0 1.9 %collective-permute-done.left = bf16[4,4,128,256]{3,2,1,0:T(8,128)(2,1)S(1)} collective-permute-done((bf16[4,4,128,256]{3,2,1,0:T(8,128)(2,1)S(1)}, bf16[4,4,128,256]{3,2,1,0:T(8,128)(2,1)S(1)}, u32[]{:S(2)}, u32[]{:S(2)}) %collective-permute-start) | collective-permute-done | bytes 1048608 | tf_op jit(solution)/shard_map/ppermute | solution.py:317
  146.9 15.0 %attention.3 = bf16[8,3,128,256]{3,2,1,0:T(8,128)(2,1)} custom-call(s32[2,8]{1,0:T(2,128)S(1)} %pad_add_fusion.meta, s32[2048,128]{1,0:T(8,128)} %broadcast_in_dim.74.marks_in, s32[1,2048]{1,0:T(1,128)S(1)} %and_select_fusion.seg_query, bf16[4,4,128,256]{3,2,1,0:T(8,128)(2,1)S(1)} %collective-permute-done.left, bf16[8,4,128,256]{3,2,1,0:T(8,128)(2,1)} %all-to-all-done.2.own, ...), custom_call_target="tpu_custom_call" | custom-call | flops 3355443200 | bytes 6291456 | tf_op jit(solution)/shard_map/attention/pallas_call | solution.py:223
  161.9 3.8 %all-to-all-start.5 = ((bf16[8,3,128,256]{3,2,1,0:T(8,128)(2,1)}), bf16[8,3,128,256]{3,2,1,0:T(8,128)(2,1)S(1)}, u32[]{:S(2)}, u32[]{:S(2)}) async-start(bf16[8,3,128,256]{3,2,1,0:T(8,128)(2,1)} %attention.3), calls=%async_computation.5 | async-start | bytes 3145728 | tf_op jit(solution)/shard_map/all_to_all | solution.py:308
  167.9 1.3 unpack.4
  169.3 16.5 %all-to-all-done.5.block = bf16[8,3,128,256]{3,2,1,0:T(8,128)(2,1)S(1)} async-done(((bf16[8,3,128,256]{3,2,1,0:T(8,128)(2,1)}), bf16[8,3,128,256]{3,2,1,0:T(8,128)(2,1)S(1)}, u32[]{:S(2)}, u32[]{:S(2)}) %all-to-all-start.5) | async-done | bytes 1572896 | tf_op jit(solution)/shard_map/all_to_all | solution.py:308
  185.8 1.3 unpack.5
  (22 shorter events, 3.7 us)
Async XLA Ops:
  3.1 18.2 %all-to-all-start = ((bf16[8,4,128,128]{3,2,1,0:T(8,128)(2,1)}), bf16[8,4,128,128]{3,2,1,0:T(8,128)(2,1)S(1)}, u32[]{:S(2)}, u32[]{:S(2)}) async-start(bf16[8,4,128,128]{3,2,1,0:T(8,128)(2,1)} %pack.5), calls=%async_computation | async-start | bytes 2097152 | tf_op jit(solution)/shard_map/all_to_all | solution.py:308
  21.3 29.2 %all-to-all-start.1 = ((bf16[8,4,128,256]{3,2,1,0:T(8,128)(2,1)}), bf16[8,4,128,256]{3,2,1,0:T(8,128)(2,1)S(1)}, u32[]{:S(2)}, u32[]{:S(2)}) async-start(bf16[8,4,128,256]{3,2,1,0:T(8,128)(2,1)} %pack.4), calls=%async_computation.1 | async-start | bytes 4194304 | tf_op jit(solution)/shard_map/all_to_all | solution.py:308
  24.9 3.2 %copy-start.2 = (s32[32]{0:T(128)S(1)}, s32[32]{0:T(128)}, u32[]{:S(2)}) copy-start(s32[32]{0:T(128)} %param.9) | copy-start | bytes 388
  50.5 34.7 %all-to-all-start.2 = ((bf16[8,4,128,256]{3,2,1,0:T(8,128)(2,1)}), bf16[8,4,128,256]{3,2,1,0:T(8,128)(2,1)}, u32[]{:S(2)}, u32[]{:S(2)}) async-start(bf16[8,4,128,256]{3,2,1,0:T(8,128)(2,1)} %pack.3), calls=%async_computation.2 | async-start | bytes 4194304 | tf_op jit(solution)/shard_map/all_to_all | solution.py:308
  55.2 16.7 %collective-permute-start.5 = (bf16[4,4,128,128]{3,2,1,0:T(8,128)(2,1)S(1)}, bf16[4,4,128,128]{3,2,1,0:T(8,128)(2,1)S(1)}, u32[]{:S(2)}, u32[]{:S(2)}) collective-permute-start(bf16[4,4,128,128]{3,2,1,0:T(8,128)(2,1)S(1)} %get-tuple-element.36), channel_id=1, source_target_pairs={{8,0},{16,8},{24,16},{9,1},{17,9},{25,17},{10,2},{18,10},{26,18},{... | collective-permute-start | bytes 1572872 | tf_op jit(solution)/shard_map/ppermute | solution.py:318
  57.6 16.7 %collective-permute-start.4 = (bf16[4,4,128,128]{3,2,1,0:T(8,128)(2,1)S(1)}, bf16[4,4,128,128]{3,2,1,0:T(8,128)(2,1)S(1)}, u32[]{:S(2)}, u32[]{:S(2)}) collective-permute-start(bf16[4,4,128,128]{3,2,1,0:T(8,128)(2,1)S(1)} %get-tuple-element.37), channel_id=1, source_target_pairs={{0,8},{8,16},{16,24},{1,9},{9,17},{17,25},{2,10},{10,18},{18,26},{... | collective-permute-start | bytes 1572872 | tf_op jit(solution)/shard_map/ppermute | solution.py:317
  62.6 31.3 %collective-permute-start.3 = (bf16[4,4,128,256]{3,2,1,0:T(8,128)(2,1)}, bf16[4,4,128,256]{3,2,1,0:T(8,128)(2,1)}, u32[]{:S(2)}, u32[]{:S(2)}) collective-permute-start(bf16[4,4,128,256]{3,2,1,0:T(8,128)(2,1)} %get-tuple-element.32), channel_id=1, source_target_pairs={{8,0},{16,8},{24,16},{9,1},{17,9},{25,17},{10,2},{18,10},{26,18},{... | collective-permute-start | bytes 3145736 | tf_op jit(solution)/shard_map/ppermute | solution.py:318
  65.0 31.0 %collective-permute-start.2 = (bf16[4,4,128,256]{3,2,1,0:T(8,128)(2,1)}, bf16[4,4,128,256]{3,2,1,0:T(8,128)(2,1)}, u32[]{:S(2)}, u32[]{:S(2)}) collective-permute-start(bf16[4,4,128,256]{3,2,1,0:T(8,128)(2,1)} %get-tuple-element.33), channel_id=1, source_target_pairs={{0,8},{8,16},{16,24},{1,9},{9,17},{17,25},{2,10},{10,18},{18,26},{... | collective-permute-start | bytes 3145736 | tf_op jit(solution)/shard_map/ppermute | solution.py:317
  85.2 25.8 %all-to-all-start.3 = ((bf16[8,3,128,128]{3,2,1,0:T(8,128)(2,1)}), bf16[8,3,128,128]{3,2,1,0:T(8,128)(2,1)S(1)}, u32[]{:S(2)}, u32[]{:S(2)}) async-start(bf16[8,3,128,128]{3,2,1,0:T(8,128)(2,1)} %attention.5), calls=%async_computation.3 | async-start | bytes 1572864 | tf_op jit(solution)/shard_map/all_to_all | solution.py:308
  111.1 0.9 copy-start
  112.0 49.9 %all-to-all-start.4 = ((bf16[8,3,128,256]{3,2,1,0:T(8,128)(2,1)}), bf16[8,3,128,256]{3,2,1,0:T(8,128)(2,1)S(1)}, u32[]{:S(2)}, u32[]{:S(2)}) async-start(bf16[8,3,128,256]{3,2,1,0:T(8,128)(2,1)} %attention.4), calls=%async_computation.4 | async-start | bytes 3145728 | tf_op jit(solution)/shard_map/all_to_all | solution.py:308
  117.5 27.5 %collective-permute-start.1 = (bf16[4,4,128,256]{3,2,1,0:T(8,128)(2,1)S(1)}, bf16[4,4,128,256]{3,2,1,0:T(8,128)(2,1)S(1)}, u32[]{:S(2)}, u32[]{:S(2)}) collective-permute-start(bf16[4,4,128,256]{3,2,1,0:T(8,128)(2,1)S(1)} %get-tuple-element.34), channel_id=1, source_target_pairs={{8,0},{16,8},{24,16},{9,1},{17,9},{25,17},{10,2},{18,10},{26,18},{... | collective-permute-start | bytes 3145736 | tf_op jit(solution)/shard_map/ppermute | solution.py:318
  119.4 27.5 %collective-permute-start = (bf16[4,4,128,256]{3,2,1,0:T(8,128)(2,1)S(1)}, bf16[4,4,128,256]{3,2,1,0:T(8,128)(2,1)S(1)}, u32[]{:S(2)}, u32[]{:S(2)}) collective-permute-start(bf16[4,4,128,256]{3,2,1,0:T(8,128)(2,1)S(1)} %get-tuple-element.35), channel_id=1, source_target_pairs={{0,8},{8,16},{16,24},{1,9},{9,17},{17,25},{2,10},{10,18},{18,26},{... | collective-permute-start | bytes 3145736 | tf_op jit(solution)/shard_map/ppermute | solution.py:317
  161.9 23.9 %all-to-all-start.5 = ((bf16[8,3,128,256]{3,2,1,0:T(8,128)(2,1)}), bf16[8,3,128,256]{3,2,1,0:T(8,128)(2,1)S(1)}, u32[]{:S(2)}, u32[]{:S(2)}) async-start(bf16[8,3,128,256]{3,2,1,0:T(8,128)(2,1)} %attention.3), calls=%async_computation.5 | async-start | bytes 3145728 | tf_op jit(solution)/shard_map/all_to_all | solution.py:308
  165.7 1.1 copy-start.1

commit v4 on v3

--- a/solution.py
+++ b/solution.py
@@ -13,10 +13,11 @@
 NEG = -1e30
 FLOOR = -1e29
 UNIT = 128
+STEP = 16
 CHUNK = 2
 TILE = 256
 STRIDE = 2
-WIDTHS = (4, 5, 6, 8, 10)
+WIDTHS = (3, 4, 5, 6, 8, 10)
 
 
 def copy_all(pairs, sems):
@@ -105,17 +106,18 @@
     sems,
     edge_sems,
 ):
-    heads, kinds, blocks, rows, _ = window.shape
-    peers = own.shape[0]
+    heads, kinds, height, _ = window.shape
+    peers, _, rows, _ = own.shape
     edge = left.shape[0]
     scale = HEAD_DIM ** (-0.5)
     factor = scale * float(np.log2(np.e))
-    unit, tall = UNIT // rows, TILE // rows
     columns = [slice(head * HEAD_DIM, (head + 1) * HEAD_DIM) for head in range(heads)]
     copies = [
         pltpu.make_async_copy(
             source.at[:, kind, :, columns[head]],
-            window.at[head, kind, first : first + source.shape[0]],
+            window.at[head, kind]
+            .reshape(height // rows, rows, HEAD_DIM)
+            .at[first : first + source.shape[0]],
             sems.at[head, kind, part],
         )
         for head in range(heads)
@@ -127,20 +129,19 @@
     copies.append(pltpu.make_async_copy(marks_in, seg_key, edge_sems.at[0]))
     for copy in copies:
         copy.start()
-    dk[...] = jnp.zeros_like(dk)
-    dv[...] = jnp.zeros_like(dv)
+    inner = slice(edge * rows, (edge + peers) * rows)
+    for head in range(heads):
+        dk[head, inner] = jnp.zeros((peers * rows, HEAD_DIM), jnp.float32)
+        dv[head, inner] = jnp.zeros((peers * rows, HEAD_DIM), jnp.float32)
     for copy in copies:
         copy.wait()
-
-    def flat(value):
-        return value.reshape(value.shape[0] * rows, HEAD_DIM)
 
     def visit(tile, width):
         lanes = pl.ds(pl.multiple_of(tile * TILE, TILE), TILE)
         first = meta[0, tile]
-        marks = seg_key[pl.ds(pl.multiple_of(first * UNIT, UNIT), width * UNIT)]
+        marks = seg_key[pl.ds(pl.multiple_of(first * STEP, STEP), width * UNIT)]
         inside = jnp.concatenate([marks] * (TILE // 128), axis=1) == seg_query[:, lanes]
-        here = pl.ds(tile * tall, tall)
+        here = lanes
         over = (((1,), (1,)), ((), ()))
         down = (((0,), (0,)), ((), ()))
         pieces = [
@@ -148,7 +149,7 @@
         ]
 
         def span(at, count):
-            return pl.ds((first + at) * unit, count * unit)
+            return pl.ds(pl.multiple_of(first * STEP + at * UNIT, STEP), count * UNIT)
 
         def dot(left, right, dims):
             return lax.dot_general(left, right, dims, preferred_element_type=jnp.float32)
@@ -156,21 +157,21 @@
         plain = (((1,), (0,)), ((), ()))
         query_terms, held = [], []
         for head in range(heads):
-            q = flat(window[head, 0, here])
+            q = window[head, 0, here]
             scores, top = [], FLOOR
             for at, count in pieces:
-                piece = dot(flat(window[head, 1, span(at, count)]), q, over)
+                piece = dot(window[head, 1, span(at, count)], q, over)
                 piece = jnp.where(inside[at * UNIT : (at + count) * UNIT], piece, NEG)
                 scores.append(piece)
                 top = jnp.maximum(top, jnp.max(piece, axis=0, keepdims=True))
             held.append((scores, top))
         middle = []
         for head in range(heads):
-            g = flat(window[head, 3, here])
+            g = window[head, 3, here]
             scores, top = held[head]
             raised, dprobs, total, product = [], [], 0.0, 0.0
             for (at, count), piece in zip(pieces, scores):
-                dprob = dot(flat(window[head, 2, span(at, count)]), g, over)
+                dprob = dot(window[head, 2, span(at, count)], g, over)
                 piece = jnp.exp2((piece - top) * factor)
                 total = total + jnp.sum(piece, axis=0, keepdims=True)
                 product = product + jnp.sum(piece * dprob, axis=0, keepdims=True)
@@ -178,7 +179,7 @@
                 dprobs.append(dprob)
             middle.append((raised, dprobs, total, product))
         for head in range(heads):
-            q, g = flat(window[head, 0, here]), flat(window[head, 3, here])
+            q, g = window[head, 0, here], window[head, 3, here]
             raised, dprobs, total, product = middle[head]
             inverse = jnp.where(total > 0.0, 1.0 / total, 0.0)
             product = product * inverse
@@ -187,11 +188,10 @@
                 probs = piece * inverse
                 dscore = (probs * (dprob - product)).astype(jnp.bfloat16)
                 keys = span(at, count)
-                shape = (count * unit, rows, HEAD_DIM)
-                dv[head, keys] += dot(probs.astype(jnp.bfloat16), g, plain).reshape(shape)
-                dk[head, keys] += dot(dscore, q, plain).reshape(shape)
-                dq = dq + dot(dscore, flat(window[head, 1, keys]), down)
-            query_terms.append((dq * scale).astype(jnp.bfloat16).reshape(tall, rows, HEAD_DIM))
+                dv[head, keys] += dot(probs.astype(jnp.bfloat16), g, plain)
+                dk[head, keys] += dot(dscore, q, plain)
+                dq = dq + dot(dscore, window[head, 1, keys], down)
+            query_terms.append((dq * scale).astype(jnp.bfloat16))
         for head in range(heads):
             grads_q[head, here] = query_terms[head]
 
@@ -200,12 +200,14 @@
             pl.when(meta[1, tile] == width)(functools.partial(visit, tile, width))
         return carry
 
-    lax.fori_loop(0, blocks // tall, step, 0)
+    lax.fori_loop(0, height // TILE, step, 0)
     for head in range(heads):
-        inner = slice(edge, edge + peers)
-        out[:, 0, :, columns[head]] = grads_q[head, inner]
-        out[:, 1, :, columns[head]] = (dk[head, inner] * scale).astype(jnp.bfloat16)
-        out[:, 2, :, columns[head]] = dv[head, inner].astype(jnp.bfloat16)
+        shape = (peers, rows, HEAD_DIM)
+        out[:, 0, :, columns[head]] = grads_q[head, inner].reshape(shape)
+        out[:, 1, :, columns[head]] = (
+            (dk[head, inner] * scale).astype(jnp.bfloat16).reshape(shape)
+        )
+        out[:, 2, :, columns[head]] = dv[head, inner].astype(jnp.bfloat16).reshape(shape)
     leaving = pltpu.make_async_copy(out, result, edge_sems.at[1])
     leaving.start()
     leaving.wait()
@@ -213,9 +215,9 @@
 
 def attention(meta, seg_key, seg_query, left, own, right, widths):
     peers, kinds, rows, width = own.shape
-    blocks = peers + 2 * left.shape[0]
+    height = (peers + 2 * left.shape[0]) * rows
     heads = width // HEAD_DIM
-    elements = heads * blocks * rows * 5 * UNIT
+    elements = heads * height * 5 * UNIT
     smem = pl.BlockSpec(memory_space=pltpu.SMEM)
     vmem = pl.BlockSpec(memory_space=pltpu.VMEM)
     outer = pl.BlockSpec(memory_space=pltpu.HBM)
@@ -228,10 +230,10 @@
         scratch_shapes=[
             pltpu.VMEM(seg_key.shape, jnp.int32),
             pltpu.VMEM((peers, 3, rows, width), jnp.bfloat16),
-            pltpu.VMEM((heads, kinds, blocks, rows, HEAD_DIM), jnp.bfloat16),
-            pltpu.VMEM((heads, blocks, rows, HEAD_DIM), jnp.bfloat16),
-            pltpu.VMEM((heads, blocks, rows, HEAD_DIM), jnp.float32),
-            pltpu.VMEM((heads, blocks, rows, HEAD_DIM), jnp.float32),
+            pltpu.VMEM((heads, kinds, height, HEAD_DIM), jnp.bfloat16),
+            pltpu.VMEM((heads, height, HEAD_DIM), jnp.bfloat16),
+            pltpu.VMEM((heads, height, HEAD_DIM), jnp.float32),
+            pltpu.VMEM((heads, height, HEAD_DIM), jnp.float32),
             pltpu.SemaphoreType.DMA((heads, kinds, 3)),
             pltpu.SemaphoreType.DMA((2,)),
         ],
@@ -267,14 +269,14 @@
     valid = touches & (at >= 0) & (at < tokens)
     seg_key = jnp.broadcast_to(jnp.where(valid, seg, -1)[:, None], (window, 128))
     seg_query = jnp.where(valid, seg, -2)[None, :]
-    first = jnp.min(jnp.where(valid, start - base, window).reshape(-1, TILE), axis=1) // UNIT
+    first = jnp.min(jnp.where(valid, start - base, window).reshape(-1, TILE), axis=1) // STEP
     last = jnp.max(jnp.where(valid, end - base, 0).reshape(-1, TILE), axis=1)
-    need = (last + UNIT - 1) // UNIT - first
+    need = (last - first * STEP + UNIT - 1) // UNIT
     chosen = jnp.full_like(need, widths[-1])
     for width in reversed(widths):
         chosen = jnp.where(need <= width, width, chosen)
     chosen = jnp.where(last > 0, chosen, 0)
-    first = jnp.clip(first, 0, window // UNIT - chosen)
+    first = jnp.clip(first, 0, (window - chosen * UNIT) // STEP)
     return jnp.stack([first, chosen]).astype(jnp.int32), seg_key, seg_query
 
 

time: 188 us -> 186 us (0.989)
  Pallas kernels: 52.3 us -> 50 us
    pallas_call x3, Pallas kernels: 39.7 us -> 37.4 us  [attention(): pl.pallas_call(functools.partial(attention_kernel, widths), in_specs=[sme...]
  transfers between devices with their start and end apart: 12 -> 12, of which waited for: 9 -> 9; matrix products, arithmetic and copies ran while one was open for 3% -> 3% of each run, Pallas kernels for 26% -> 25%
where the time goes in v4:
time: 186 us; the launch traced here: 185 us
  waiting for transfers between devices  85.9 us (46%)
  Pallas kernels  50 us (27%)
  starting transfers between devices  41.2 us (22%)
  local copies, waits for them, and re-layouts  6.62 us (4%)
    all_to_all x6, waiting for transfers between devices, exchange(): return lax.all_to_all(block, plane, split_axis=0, concat_axis=0, tiled=True)  49.9 us
    pallas_call x3, Pallas kernels, attention(): pl.pallas_call(functools.partial(attention_kernel, widths), in_specs=[sme...  37.4 us
    ppermute x3, waiting for transfers between devices, shards(): right = lax.ppermute(own[:edge], 'g', down)  29.6 us
    all_to_all x6, starting transfers between devices, exchange(): return lax.all_to_all(block, plane, split_axis=0, concat_axis=0, tiled=True)  23.4 us
    ppermute x3, starting transfers between devices, shards(): left = lax.ppermute(own[peers - edge:], 'g', up)  11.1 us
    pallas_call x3, Pallas kernels, pack(): pl.pallas_call(functools.partial(pack_kernel, first, count), in_specs=[an...  8.82 us
    ppermute x3, starting transfers between devices, shards(): right = lax.ppermute(own[:edge], 'g', down)  6.65 us
    ppermute x3, waiting for transfers between devices, shards(): left = lax.ppermute(own[peers - edge:], 'g', up)  6.38 us
  transfers between devices with their start and end apart: 12, of which 9 were waited for; matrix products, arithmetic and copies ran while one was open for 3% of the time, Pallas kernels for 25%

profile of v4, /device:TPU:8, one launch (start us, length us, event | category | flops | bytes accessed | tf_op | source)
XLA Modules:
  0.0 185.3 jit_solution(11423142003349374437)
XLA Ops:
  0.6 2.4 %pack.5 = bf16[8,4,128,128]{3,2,1,0:T(8,128)(2,1)} custom-call(bf16[128,5120]{1,0:T(8,128)(2,1)} %refs_0_.5, bf16[128,5120]{1,0:T(8,128)(2,1)} %refs_1_.5, bf16[128,5120]{1,0:T(8,128)(2,1)} %refs_2_.5, bf16[128,5120]{1,0:T(8,128)(2,1)} %refs_3_.5), custom_call_target="tpu_custom_call" | custom-call | tf_op jit(solution)/shard_map/pack/pallas_call | solution.py:52
  3.1 3.7 %all-to-all-start = ((bf16[8,4,128,128]{3,2,1,0:T(8,128)(2,1)}), bf16[8,4,128,128]{3,2,1,0:T(8,128)(2,1)S(1)}, u32[]{:S(2)}, u32[]{:S(2)}) async-start(bf16[8,4,128,128]{3,2,1,0:T(8,128)(2,1)} %pack.5), calls=%async_computation | async-start | bytes 2097152 | tf_op jit(solution)/shard_map/all_to_all | solution.py:310
  6.8 3.2 %pack.4 = bf16[8,4,128,256]{3,2,1,0:T(8,128)(2,1)} custom-call(bf16[128,5120]{1,0:T(8,128)(2,1)} %refs_0_.5, bf16[128,5120]{1,0:T(8,128)(2,1)} %refs_1_.5, bf16[128,5120]{1,0:T(8,128)(2,1)} %refs_2_.5, bf16[128,5120]{1,0:T(8,128)(2,1)} %refs_3_.5), custom_call_target="tpu_custom_call" | custom-call | tf_op jit(solution)/shard_map/pack/pallas_call | solution.py:52
  10.0 11.3 %all-to-all-done.own = bf16[8,4,128,128]{3,2,1,0:T(8,128)(2,1)S(1)} async-done(((bf16[8,4,128,128]{3,2,1,0:T(8,128)(2,1)}), bf16[8,4,128,128]{3,2,1,0:T(8,128)(2,1)S(1)}, u32[]{:S(2)}, u32[]{:S(2)}) %all-to-all-start) | async-done | bytes 1048608 | tf_op jit(solution)/shard_map/all_to_all | solution.py:310
  21.3 3.6 %all-to-all-start.1 = ((bf16[8,4,128,256]{3,2,1,0:T(8,128)(2,1)}), bf16[8,4,128,256]{3,2,1,0:T(8,128)(2,1)S(1)}, u32[]{:S(2)}, u32[]{:S(2)}) async-start(bf16[8,4,128,256]{3,2,1,0:T(8,128)(2,1)} %pack.4), calls=%async_computation.1 | async-start | bytes 4194304 | tf_op jit(solution)/shard_map/all_to_all | solution.py:310
  24.9 3.2 %pack.3 = bf16[8,4,128,256]{3,2,1,0:T(8,128)(2,1)} custom-call(bf16[128,5120]{1,0:T(8,128)(2,1)} %refs_0_.5, bf16[128,5120]{1,0:T(8,128)(2,1)} %refs_1_.5, bf16[128,5120]{1,0:T(8,128)(2,1)} %refs_2_.5, bf16[128,5120]{1,0:T(8,128)(2,1)} %refs_3_.5), custom_call_target="tpu_custom_call" | custom-call | tf_op jit(solution)/shard_map/pack/pallas_call | solution.py:52
  28.4 22.1 %all-to-all-done.1.own = bf16[8,4,128,256]{3,2,1,0:T(8,128)(2,1)S(1)} async-done(((bf16[8,4,128,256]{3,2,1,0:T(8,128)(2,1)}), bf16[8,4,128,256]{3,2,1,0:T(8,128)(2,1)S(1)}, u32[]{:S(2)}, u32[]{:S(2)}) %all-to-all-start.1) | async-done | bytes 2097184 | tf_op jit(solution)/shard_map/all_to_all | solution.py:310
  50.5 4.4 %all-to-all-start.2 = ((bf16[8,4,128,256]{3,2,1,0:T(8,128)(2,1)}), bf16[8,4,128,256]{3,2,1,0:T(8,128)(2,1)}, u32[]{:S(2)}, u32[]{:S(2)}) async-start(bf16[8,4,128,256]{3,2,1,0:T(8,128)(2,1)} %pack.3), calls=%async_computation.2 | async-start | bytes 4194304 | tf_op jit(solution)/shard_map/all_to_all | solution.py:310
  55.2 2.4 %collective-permute-start.5 = (bf16[4,4,128,128]{3,2,1,0:T(8,128)(2,1)S(1)}, bf16[4,4,128,128]{3,2,1,0:T(8,128)(2,1)S(1)}, u32[]{:S(2)}, u32[]{:S(2)}) collective-permute-start(bf16[4,4,128,128]{3,2,1,0:T(8,128)(2,1)S(1)} %get-tuple-element.36), channel_id=1, source_target_pairs={{8,0},{16,8},{24,16},{9,1},{17,9},{25,17},{10,2},{18,10},{26,18},{... | collective-permute-start | bytes 1572872 | tf_op jit(solution)/shard_map/ppermute | solution.py:320
  57.6 3.5 %collective-permute-start.4 = (bf16[4,4,128,128]{3,2,1,0:T(8,128)(2,1)S(1)}, bf16[4,4,128,128]{3,2,1,0:T(8,128)(2,1)S(1)}, u32[]{:S(2)}, u32[]{:S(2)}) collective-permute-start(bf16[4,4,128,128]{3,2,1,0:T(8,128)(2,1)S(1)} %get-tuple-element.37), channel_id=1, source_target_pairs={{0,8},{8,16},{16,24},{1,9},{9,17},{17,25},{2,10},{10,18},{18,26},{... | collective-permute-start | bytes 1572872 | tf_op jit(solution)/shard_map/ppermute | solution.py:319
  61.1 1.5 fusion.8
  62.6 2.4 %collective-permute-start.3 = (bf16[4,4,128,256]{3,2,1,0:T(8,128)(2,1)}, bf16[4,4,128,256]{3,2,1,0:T(8,128)(2,1)}, u32[]{:S(2)}, u32[]{:S(2)}) collective-permute-start(bf16[4,4,128,256]{3,2,1,0:T(8,128)(2,1)} %get-tuple-element.32), channel_id=1, source_target_pairs={{8,0},{16,8},{24,16},{9,1},{17,9},{25,17},{10,2},{18,10},{26,18},{... | collective-permute-start | bytes 3145736 | tf_op jit(solution)/shard_map/ppermute | solution.py:320
  65.0 3.5 %collective-permute-start.2 = (bf16[4,4,128,256]{3,2,1,0:T(8,128)(2,1)}, bf16[4,4,128,256]{3,2,1,0:T(8,128)(2,1)}, u32[]{:S(2)}, u32[]{:S(2)}) collective-permute-start(bf16[4,4,128,256]{3,2,1,0:T(8,128)(2,1)} %get-tuple-element.33), channel_id=1, source_target_pairs={{0,8},{8,16},{16,24},{1,9},{9,17},{17,25},{2,10},{10,18},{18,26},{... | collective-permute-start | bytes 3145736 | tf_op jit(solution)/shard_map/ppermute | solution.py:319
  68.5 3.4 %collective-permute-done.5.right = bf16[4,4,128,128]{3,2,1,0:T(8,128)(2,1)S(1)} collective-permute-done((bf16[4,4,128,128]{3,2,1,0:T(8,128)(2,1)S(1)}, bf16[4,4,128,128]{3,2,1,0:T(8,128)(2,1)S(1)}, u32[]{:S(2)}, u32[]{:S(2)}) %collective-permute-start.5) | collective-permute-done | bytes 524320 | tf_op jit(solution)/shard_map/ppermute | solution.py:320
  71.9 2.4 %collective-permute-done.4.left = bf16[4,4,128,128]{3,2,1,0:T(8,128)(2,1)S(1)} collective-permute-done((bf16[4,4,128,128]{3,2,1,0:T(8,128)(2,1)S(1)}, bf16[4,4,128,128]{3,2,1,0:T(8,128)(2,1)S(1)}, u32[]{:S(2)}, u32[]{:S(2)}) %collective-permute-start.4) | collective-permute-done | bytes 524320 | tf_op jit(solution)/shard_map/ppermute | solution.py:319
  74.3 1.3 broadcast_in_dim.75.marks_in
  75.6 9.3 %attention.5 = bf16[8,3,128,128]{3,2,1,0:T(8,128)(2,1)} custom-call(s32[2,8]{1,0:T(2,128)S(1)} %pad_add_fusion.meta, s32[2048,128]{1,0:T(8,128)} %broadcast_in_dim.75.marks_in, s32[1,2048]{1,0:T(1,128)S(1)} %and_select_fusion.seg_query, bf16[4,4,128,128]{3,2,1,0:T(8,128)(2,1)S(1)} %collective-permute-done.4.left, ...), custom_call_target="tpu_custom_call" | custom-call | flops 1677721600 | bytes 3145728 | tf_op jit(solution)/shard_map/attention/pallas_call | solution.py:225
  85.0 4.1 %all-to-all-start.3 = ((bf16[8,3,128,128]{3,2,1,0:T(8,128)(2,1)}), bf16[8,3,128,128]{3,2,1,0:T(8,128)(2,1)S(1)}, u32[]{:S(2)}, u32[]{:S(2)}) async-start(bf16[8,3,128,128]{3,2,1,0:T(8,128)(2,1)} %attention.5), calls=%async_computation.3 | async-start | bytes 1572864 | tf_op jit(solution)/shard_map/all_to_all | solution.py:310
  89.0 4.9 %collective-permute-done.3.right = bf16[4,4,128,256]{3,2,1,0:T(8,128)(2,1)} collective-permute-done((bf16[4,4,128,256]{3,2,1,0:T(8,128)(2,1)}, bf16[4,4,128,256]{3,2,1,0:T(8,128)(2,1)}, u32[]{:S(2)}, u32[]{:S(2)}) %collective-permute-start.3) | collective-permute-done | bytes 1048608 | tf_op jit(solution)/shard_map/ppermute | solution.py:320
  93.9 2.1 %collective-permute-done.2.left = bf16[4,4,128,256]{3,2,1,0:T(8,128)(2,1)} collective-permute-done((bf16[4,4,128,256]{3,2,1,0:T(8,128)(2,1)}, bf16[4,4,128,256]{3,2,1,0:T(8,128)(2,1)}, u32[]{:S(2)}, u32[]{:S(2)}) %collective-permute-start.2) | collective-permute-done | bytes 1048608 | tf_op jit(solution)/shard_map/ppermute | solution.py:319
  96.0 14.1 %attention.4 = bf16[8,3,128,256]{3,2,1,0:T(8,128)(2,1)} custom-call(s32[2,8]{1,0:T(2,128)S(1)} %pad_add_fusion.meta, s32[2048,128]{1,0:T(8,128)} %broadcast_in_dim.75.marks_in, s32[1,2048]{1,0:T(1,128)S(1)} %and_select_fusion.seg_query, bf16[4,4,128,256]{3,2,1,0:T(8,128)(2,1)} %collective-permute-done.2.left, ...), custom_call_target="tpu_custom_call" | custom-call | flops 3355443200 | bytes 6291456 | tf_op jit(solution)/shard_map/attention/pallas_call | solution.py:225
  111.0 3.8 %all-to-all-start.4 = ((bf16[8,3,128,256]{3,2,1,0:T(8,128)(2,1)}), bf16[8,3,128,256]{3,2,1,0:T(8,128)(2,1)S(1)}, u32[]{:S(2)}, u32[]{:S(2)}) async-start(bf16[8,3,128,256]{3,2,1,0:T(8,128)(2,1)} %attention.4), calls=%async_computation.4 | async-start | bytes 3145728 | tf_op jit(solution)/shard_map/all_to_all | solution.py:310
  114.8 1.7 fusion.9
  116.5 1.9 %collective-permute-start.1 = (bf16[4,4,128,256]{3,2,1,0:T(8,128)(2,1)S(1)}, bf16[4,4,128,256]{3,2,1,0:T(8,128)(2,1)S(1)}, u32[]{:S(2)}, u32[]{:S(2)}) collective-permute-start(bf16[4,4,128,256]{3,2,1,0:T(8,128)(2,1)S(1)} %get-tuple-element.34), channel_id=1, source_target_pairs={{8,0},{16,8},{24,16},{9,1},{17,9},{25,17},{10,2},{18,10},{26,18},{... | collective-permute-start | bytes 3145736 | tf_op jit(solution)/shard_map/ppermute | solution.py:320
  118.4 4.1 %collective-permute-start = (bf16[4,4,128,256]{3,2,1,0:T(8,128)(2,1)S(1)}, bf16[4,4,128,256]{3,2,1,0:T(8,128)(2,1)S(1)}, u32[]{:S(2)}, u32[]{:S(2)}) collective-permute-start(bf16[4,4,128,256]{3,2,1,0:T(8,128)(2,1)S(1)} %get-tuple-element.35), channel_id=1, source_target_pairs={{0,8},{8,16},{16,24},{1,9},{9,17},{17,25},{2,10},{10,18},{18,26},{... | collective-permute-start | bytes 3145736 | tf_op jit(solution)/shard_map/ppermute | solution.py:319
  122.6 21.4 %collective-permute-done.1.right = bf16[4,4,128,256]{3,2,1,0:T(8,128)(2,1)S(1)} collective-permute-done((bf16[4,4,128,256]{3,2,1,0:T(8,128)(2,1)S(1)}, bf16[4,4,128,256]{3,2,1,0:T(8,128)(2,1)S(1)}, u32[]{:S(2)}, u32[]{:S(2)}) %collective-permute-start.1) | collective-permute-done | bytes 1048608 | tf_op jit(solution)/shard_map/ppermute | solution.py:320
  144.0 1.9 %collective-permute-done.left = bf16[4,4,128,256]{3,2,1,0:T(8,128)(2,1)S(1)} collective-permute-done((bf16[4,4,128,256]{3,2,1,0:T(8,128)(2,1)S(1)}, bf16[4,4,128,256]{3,2,1,0:T(8,128)(2,1)S(1)}, u32[]{:S(2)}, u32[]{:S(2)}) %collective-permute-start) | collective-permute-done | bytes 1048608 | tf_op jit(solution)/shard_map/ppermute | solution.py:319
  145.9 14.0 %attention.3 = bf16[8,3,128,256]{3,2,1,0:T(8,128)(2,1)} custom-call(s32[2,8]{1,0:T(2,128)S(1)} %pad_add_fusion.meta, s32[2048,128]{1,0:T(8,128)} %broadcast_in_dim.75.marks_in, s32[1,2048]{1,0:T(1,128)S(1)} %and_select_fusion.seg_query, bf16[4,4,128,256]{3,2,1,0:T(8,128)(2,1)S(1)} %collective-permute-done.left, bf16[8,4,128,256]{3,2,1,0:T(8,128)(2,1)} %all-to-all-done.2.own, ...), custom_call_target="tpu_custom_call" | custom-call | flops 3355443200 | bytes 6291456 | tf_op jit(solution)/shard_map/attention/pallas_call | solution.py:225
  159.9 3.8 %all-to-all-start.5 = ((bf16[8,3,128,256]{3,2,1,0:T(8,128)(2,1)}), bf16[8,3,128,256]{3,2,1,0:T(8,128)(2,1)S(1)}, u32[]{:S(2)}, u32[]{:S(2)}) async-start(bf16[8,3,128,256]{3,2,1,0:T(8,128)(2,1)} %attention.3), calls=%async_computation.5 | async-start | bytes 3145728 | tf_op jit(solution)/shard_map/all_to_all | solution.py:310
  165.9 1.3 unpack.4
  167.3 16.5 %all-to-all-done.5.block = bf16[8,3,128,256]{3,2,1,0:T(8,128)(2,1)S(1)} async-done(((bf16[8,3,128,256]{3,2,1,0:T(8,128)(2,1)}), bf16[8,3,128,256]{3,2,1,0:T(8,128)(2,1)S(1)}, u32[]{:S(2)}, u32[]{:S(2)}) %all-to-all-start.5) | async-done | bytes 1572896 | tf_op jit(solution)/shard_map/all_to_all | solution.py:310
  183.8 1.3 unpack.5
  (22 shorter events, 3.7 us)
Async XLA Ops:
  3.1 18.2 %all-to-all-start = ((bf16[8,4,128,128]{3,2,1,0:T(8,128)(2,1)}), bf16[8,4,128,128]{3,2,1,0:T(8,128)(2,1)S(1)}, u32[]{:S(2)}, u32[]{:S(2)}) async-start(bf16[8,4,128,128]{3,2,1,0:T(8,128)(2,1)} %pack.5), calls=%async_computation | async-start | bytes 2097152 | tf_op jit(solution)/shard_map/all_to_all | solution.py:310
  21.3 29.2 %all-to-all-start.1 = ((bf16[8,4,128,256]{3,2,1,0:T(8,128)(2,1)}), bf16[8,4,128,256]{3,2,1,0:T(8,128)(2,1)S(1)}, u32[]{:S(2)}, u32[]{:S(2)}) async-start(bf16[8,4,128,256]{3,2,1,0:T(8,128)(2,1)} %pack.4), calls=%async_computation.1 | async-start | bytes 4194304 | tf_op jit(solution)/shard_map/all_to_all | solution.py:310
  24.9 3.2 %copy-start.2 = (s32[32]{0:T(128)S(1)}, s32[32]{0:T(128)}, u32[]{:S(2)}) copy-start(s32[32]{0:T(128)} %param.9) | copy-start | bytes 388
  50.5 34.4 %all-to-all-start.2 = ((bf16[8,4,128,256]{3,2,1,0:T(8,128)(2,1)}), bf16[8,4,128,256]{3,2,1,0:T(8,128)(2,1)}, u32[]{:S(2)}, u32[]{:S(2)}) async-start(bf16[8,4,128,256]{3,2,1,0:T(8,128)(2,1)} %pack.3), calls=%async_computation.2 | async-start | bytes 4194304 | tf_op jit(solution)/shard_map/all_to_all | solution.py:310
  55.2 16.7 %collective-permute-start.5 = (bf16[4,4,128,128]{3,2,1,0:T(8,128)(2,1)S(1)}, bf16[4,4,128,128]{3,2,1,0:T(8,128)(2,1)S(1)}, u32[]{:S(2)}, u32[]{:S(2)}) collective-permute-start(bf16[4,4,128,128]{3,2,1,0:T(8,128)(2,1)S(1)} %get-tuple-element.36), channel_id=1, source_target_pairs={{8,0},{16,8},{24,16},{9,1},{17,9},{25,17},{10,2},{18,10},{26,18},{... | collective-permute-start | bytes 1572872 | tf_op jit(solution)/shard_map/ppermute | solution.py:320
  57.6 16.7 %collective-permute-start.4 = (bf16[4,4,128,128]{3,2,1,0:T(8,128)(2,1)S(1)}, bf16[4,4,128,128]{3,2,1,0:T(8,128)(2,1)S(1)}, u32[]{:S(2)}, u32[]{:S(2)}) collective-permute-start(bf16[4,4,128,128]{3,2,1,0:T(8,128)(2,1)S(1)} %get-tuple-element.37), channel_id=1, source_target_pairs={{0,8},{8,16},{16,24},{1,9},{9,17},{17,25},{2,10},{10,18},{18,26},{... | collective-permute-start | bytes 1572872 | tf_op jit(solution)/shard_map/ppermute | solution.py:319
  62.6 31.3 %collective-permute-start.3 = (bf16[4,4,128,256]{3,2,1,0:T(8,128)(2,1)}, bf16[4,4,128,256]{3,2,1,0:T(8,128)(2,1)}, u32[]{:S(2)}, u32[]{:S(2)}) collective-permute-start(bf16[4,4,128,256]{3,2,1,0:T(8,128)(2,1)} %get-tuple-element.32), channel_id=1, source_target_pairs={{8,0},{16,8},{24,16},{9,1},{17,9},{25,17},{10,2},{18,10},{26,18},{... | collective-permute-start | bytes 3145736 | tf_op jit(solution)/shard_map/ppermute | solution.py:320
  65.0 31.0 %collective-permute-start.2 = (bf16[4,4,128,256]{3,2,1,0:T(8,128)(2,1)}, bf16[4,4,128,256]{3,2,1,0:T(8,128)(2,1)}, u32[]{:S(2)}, u32[]{:S(2)}) collective-permute-start(bf16[4,4,128,256]{3,2,1,0:T(8,128)(2,1)} %get-tuple-element.33), channel_id=1, source_target_pairs={{0,8},{8,16},{16,24},{1,9},{9,17},{17,25},{2,10},{10,18},{18,26},{... | collective-permute-start | bytes 3145736 | tf_op jit(solution)/shard_map/ppermute | solution.py:319
  85.0 25.1 %all-to-all-start.3 = ((bf16[8,3,128,128]{3,2,1,0:T(8,128)(2,1)}), bf16[8,3,128,128]{3,2,1,0:T(8,128)(2,1)S(1)}, u32[]{:S(2)}, u32[]{:S(2)}) async-start(bf16[8,3,128,128]{3,2,1,0:T(8,128)(2,1)} %attention.5), calls=%async_computation.3 | async-start | bytes 1572864 | tf_op jit(solution)/shard_map/all_to_all | solution.py:310
  110.1 0.9 copy-start
  111.0 49.0 %all-to-all-start.4 = ((bf16[8,3,128,256]{3,2,1,0:T(8,128)(2,1)}), bf16[8,3,128,256]{3,2,1,0:T(8,128)(2,1)S(1)}, u32[]{:S(2)}, u32[]{:S(2)}) async-start(bf16[8,3,128,256]{3,2,1,0:T(8,128)(2,1)} %attention.4), calls=%async_computation.4 | async-start | bytes 3145728 | tf_op jit(solution)/shard_map/all_to_all | solution.py:310
  116.5 27.5 %collective-permute-start.1 = (bf16[4,4,128,256]{3,2,1,0:T(8,128)(2,1)S(1)}, bf16[4,4,128,256]{3,2,1,0:T(8,128)(2,1)S(1)}, u32[]{:S(2)}, u32[]{:S(2)}) collective-permute-start(bf16[4,4,128,256]{3,2,1,0:T(8,128)(2,1)S(1)} %get-tuple-element.34), channel_id=1, source_target_pairs={{8,0},{16,8},{24,16},{9,1},{17,9},{25,17},{10,2},{18,10},{26,18},{... | collective-permute-start | bytes 3145736 | tf_op jit(solution)/shard_map/ppermute | solution.py:320
  118.4 27.5 %collective-permute-start = (bf16[4,4,128,256]{3,2,1,0:T(8,128)(2,1)S(1)}, bf16[4,4,128,256]{3,2,1,0:T(8,128)(2,1)S(1)}, u32[]{:S(2)}, u32[]{:S(2)}) collective-permute-start(bf16[4,4,128,256]{3,2,1,0:T(8,128)(2,1)S(1)} %get-tuple-element.35), channel_id=1, source_target_pairs={{0,8},{8,16},{16,24},{1,9},{9,17},{17,25},{2,10},{10,18},{18,26},{... | collective-permute-start | bytes 3145736 | tf_op jit(solution)/shard_map/ppermute | solution.py:319
  159.9 23.9 %all-to-all-start.5 = ((bf16[8,3,128,256]{3,2,1,0:T(8,128)(2,1)}), bf16[8,3,128,256]{3,2,1,0:T(8,128)(2,1)S(1)}, u32[]{:S(2)}, u32[]{:S(2)}) async-start(bf16[8,3,128,256]{3,2,1,0:T(8,128)(2,1)} %attention.3), calls=%async_computation.5 | async-start | bytes 3145728 | tf_op jit(solution)/shard_map/all_to_all | solution.py:310
  163.7 1.1 copy-start.1
